TPU v7x, 512 devices: a whole 4x8x8 slice. The times are simulated.
512 devices in a mesh: dom: 128 (over y, z, core), grp: 4 (over x).
Axes of the slice: x: 4, y: 8, z: 8, core: 2. Of those that a mesh axis runs over, the one named last changes fastest.
Arguments:
- right_side: float32 [512, 2, 80, 128], P(('dom', 'grp')), may hold values from -24 to 24
- absorption: float32 [512, 80, 128], P(('dom', 'grp')), may hold values from 0.5 to 4
- vertical: float32 [512, 2, 80, 128], P(('dom', 'grp')), may hold values from -1.5 to 0.3
- horizontal: float32 [512, 6, 80, 128], P(('dom', 'grp')), may hold values from -1 to 0.25
- neighbours: int32 [512, 6, 128], P(('dom', 'grp')), may hold values from 0 to 256, as said below
- send_index: int32 [512, 8, 16], P(('dom', 'grp')), may hold values from 0 to 127
- aggregate: int32 [512, 128], P(('dom', 'grp')), may hold values from 0 to 15, as said below
- weights: float32 [512, 80, 128], P(('dom', 'grp')), may hold values from 0.5 to 1.5
- coarse_vertical: float32 [512, 2, 80, 16], P(('dom', 'grp')), may hold values from -1.5 to 0.3
- coarse_horizontal: float32 [512, 6, 80, 16], P(('dom', 'grp')), may hold values from -1 to 0.25
- coarse_neighbours: int32 [512, 6, 16], P(('dom', 'grp')), may hold values from 0 to 144, as said below
Outputs:
- solution: float32 [512, 2, 80, 128], P(('dom', 'grp'))
Inputs may be any that keep to these rules, and one draw needn't show every extreme that they name: `neighbours`: below 128 an entry names a column of the same partition (never the column itself); from 128 to 255 it names column i of ghost slot s as 128 + s * 16 + i; 256 is a padded slot that reads a zero cell. Each column has 3 to 6 live slots, the live ones first. `aggregate`: every coarse column of a partition has at least one fine column. `coarse_neighbours`: an entry (k + 4) * 16 + j names coarse column j of the partition k places away, k from -4 to 4, never the column itself; (9) * 16 is a padded slot that reads a zero cell. Each coarse column has 2 to 6 live slots, the live ones first.
All inputs are finite; a program needn't handle non-finite values.
Results may differ from a plain program's by a relative error of at most 0.0001.
Values sent between devices are 32-bit elements; how exact they have to be, the bound alone decides.
A program may use at most 64 MiB of HBM per device.

v0:
```python
import jax
import jax.numpy as jnp
from jax import lax
from jax.sharding import PartitionSpec as P

CYCLES = 2
PRE = 2
POST = 2
CSWEEPS = 4


OMEGA = 0.8


def from_behind(block, axis, distance):
    devices = range(lax.axis_size(axis))
    route = [(i - distance, i) for i in devices if i - distance in devices]
    return lax.ppermute(block, axis, route)


def layer_pair(tracer_field):
    zero_rim = jnp.zeros_like(tracer_field[:, :1])
    lower_layer = jnp.concatenate([zero_rim, tracer_field[:, :-1]], 1)
    upper_layer = jnp.concatenate([tracer_field[:, 1:], zero_rim], 1)
    return (lower_layer, upper_layer)


def apply_rows(tracer_field, extended, diagonal, vertical, horizontal, neighbours):
    lower_layer, upper_layer = layer_pair(tracer_field)
    totals = diagonal * tracer_field + vertical[0] * lower_layer + vertical[1] * upper_layer
    for branch in range(neighbours.shape[0]):
        totals = totals + horizontal[branch] * jnp.take(extended, neighbours[branch], axis=2)
    return totals


def body(
    right_side,
    absorption,
    vertical,
    horizontal,
    neighbours,
    send_index,
    aggregate,
    weights,
    coarse_vertical,
    coarse_horizontal,
    coarse_neighbours,
):
    source_rhs = right_side[0]
    vertical_rows = vertical[0]
    horizontal_rows = horizontal[0]
    neighbour_rows = neighbours[0]
    weight_rows = weights[0]
    diagonal = (
        absorption[0]
        + jnp.abs(vertical_rows[0])
        + jnp.abs(vertical_rows[1])
        + jnp.sum(jnp.abs(horizontal_rows), axis=0)
    )
    reach = send_index.shape[1] // 2
    width = send_index.shape[2]
    offsets = list(range(1, reach + 1)) + [-distance for distance in range(1, reach + 1)]
    send_flat = send_index[0].reshape(-1)
    tracers, layers, columns = source_rhs.shape
    coarse_count = coarse_neighbours.shape[2]
    one_hot = (aggregate[0][:, None] == jnp.arange(coarse_count, dtype=jnp.int32)[None, :]).astype(
        jnp.float32
    )
    zero_column = jnp.zeros((tracers, layers, 1), jnp.float32)

    def ghost_blocks(tracer_field):
        packed = jnp.take(tracer_field, send_flat, axis=2)
        received = []
        for position, offset in enumerate(offsets):
            piece = packed[:, :, position * width : (position + 1) * width]
            received.append(from_behind(piece, ("dom", "grp"), offset))
        return received

    def fine_apply(tracer_field):
        extended = jnp.concatenate([tracer_field] + ghost_blocks(tracer_field) + [zero_column], 2)
        return apply_rows(
            tracer_field, extended, diagonal, vertical_rows, horizontal_rows, neighbour_rows
        )

    group_size = lax.axis_size("grp")
    group_vertical, group_horizontal = (
        lax.all_gather(coarse_vertical, "grp", axis=0, tiled=True),
        lax.all_gather(coarse_horizontal, "grp", axis=0, tiled=True),
    )
    group_neighbours = lax.all_gather(coarse_neighbours, "grp", axis=0, tiled=True)
    group_diagonal = (
        0.5
        + jnp.abs(group_vertical[:, 0])
        + jnp.abs(group_vertical[:, 1])
        + jnp.sum(jnp.abs(group_horizontal), axis=1)
    )
    member = lax.axis_index("grp")
    solution = OMEGA * source_rhs / diagonal
    for cycle_index in range(CYCLES):
        for sweep_index in range(PRE):
            if cycle_index == 0 and sweep_index == 0:
                solution = OMEGA * source_rhs / diagonal
            else:
                solution = solution + OMEGA * (source_rhs - fine_apply(solution)) / diagonal
        residual = source_rhs - fine_apply(solution)
        coarse_source = jnp.dot(
            (residual * weight_rows).reshape(tracers * layers, columns),
            one_hot,
            precision=lax.Precision.HIGHEST,
            preferred_element_type=jnp.float32,
        ).reshape(tracers, layers, coarse_count)
        group_source = lax.all_gather(coarse_source[None], "grp", axis=0, tiled=True)
        correction = OMEGA * group_source / group_diagonal[:, None]
        for coarse_sweep_index in range(CSWEEPS - 1):
            sides = [from_behind(correction, "dom", amount) for amount in (1, -1)]
            beside_all = jnp.concatenate([sides[0], correction, sides[1]], 0)
            images = []
            for index_member in range(group_size):
                window = beside_all[
                    index_member + group_size - reach : index_member + group_size + reach + 1
                ]
                flattened = jnp.transpose(window, (1, 2, 0, 3)).reshape(tracers, layers, -1)
                coarse_extended = jnp.concatenate([flattened, zero_column], 2)
                images.append(
                    apply_rows(
                        correction[index_member],
                        coarse_extended,
                        group_diagonal[index_member],
                        group_vertical[index_member],
                        group_horizontal[index_member],
                        group_neighbours[index_member],
                    )
                )
            correction = (
                correction + OMEGA * (group_source - jnp.stack(images)) / group_diagonal[:, None]
            )
        correction = lax.dynamic_index_in_dim(correction, member, 0, keepdims=False)
        lifted = jnp.dot(
            correction.reshape(tracers * layers, coarse_count),
            one_hot.T,
            precision=lax.Precision.HIGHEST,
            preferred_element_type=jnp.float32,
        ).reshape(tracers, layers, columns)
        solution = solution + lifted * weight_rows
        for sweep_index in range(POST):
            solution = solution + OMEGA * (source_rhs - fine_apply(solution)) / diagonal
    return solution[None]


def solution(mesh):
    placed = (
        P(("dom", "grp"), None, None, None),
        P(("dom", "grp"), None, None),
        P(("dom", "grp"), None, None, None),
        P(("dom", "grp"), None, None, None),
        P(("dom", "grp"), None, None),
        P(("dom", "grp"), None, None),
        P(("dom", "grp"), None),
        P(("dom", "grp"), None, None),
        P(("dom", "grp"), None, None, None),
        P(("dom", "grp"), None, None, None),
        P(("dom", "grp"), None, None),
    )
    return jax.shard_map(
        body,
        mesh=mesh,
        in_specs=placed,
        out_specs=P(("dom", "grp"), None, None, None),
        check_vma=False,
    )
```

profile of v0, /device:TPU:32, one launch (start us, length us, event | category | flops | bytes accessed | tf_op | source)
XLA Modules:
  0.0 570.7 jit_solution(5829197177640350718)
XLA Ops:
  19.0 6.2 %collective-permute-start.4 = (f32[2,80,16]{2,1,0:T(8,128)S(1)}, f32[2,80,16]{2,1,0:T(8,128)S(1)}, u32[]{:S(2)}, u32[]{:S(2)}) collective-permute-start(f32[2,80,16]{2,1,0:T(8,128)S(1)} %get-tuple-element.209), channel_id=1, source_target_pairs={{1,0},{2,1},{3,2},{4,3},{5,4},{6,5},{7,6},{8,7},{9,8},{10,9},{11,1... | collective-permute-start | bytes 30728 | tf_op jit(solution)/shard_map/ppermute | solution.py:18
  25.9 12.1 %all_gather.18 = s32[4,6,16]{2,1,0:T(8,128)S(1)} all-gather(s32[1,6,16]{2,1,0:T(8,128)S(1)} %copy.406), channel_id=1, replica_groups=mesh['dom'=128,'grp'=4] {'grp'}, dimensions={0}, use_global_device_ids=true | all-gather | bytes 1920 | tf_op jit(solution)/shard_map/all_gather | solution.py:90
  38.0 12.2 %all_gather.17 = f32[4,6,80,16]{2,3,1,0:T(8,128)S(1)} all-gather(f32[1,6,80,16]{2,3,1,0:T(8,128)S(1)} %copy-done.4), channel_id=1, replica_groups=mesh['dom'=128,'grp'=4] {'grp'}, dimensions={0}, use_global_device_ids=true | all-gather | bytes 153600 | tf_op jit(solution)/shard_map/all_gather | solution.py:88
  51.0 11.9 %all_gather.16 = f32[4,2,80,16]{2,3,1,0:T(8,128)S(1)} all-gather(f32[1,2,80,16]{2,3,1,0:T(8,128)S(1)} %copy-done.6), channel_id=1, replica_groups=mesh['dom'=128,'grp'=4] {'grp'}, dimensions={0}, use_global_device_ids=true | all-gather | bytes 51200 | tf_op jit(solution)/shard_map/all_gather | solution.py:87
  65.1 6.0 %collective-permute-start.6 = (f32[2,80,16]{2,1,0:T(8,128)S(1)}, f32[2,80,16]{2,1,0:T(8,128)S(1)}, u32[]{:S(2)}, u32[]{:S(2)}) collective-permute-start(f32[2,80,16]{2,1,0:T(8,128)S(1)} %get-tuple-element.207), channel_id=1, source_target_pairs={{3,0},{4,1},{5,2},{6,3},{7,4},{8,5},{9,6},{10,7},{11,8},{12,9},{13... | collective-permute-start | bytes 30728 | tf_op jit(solution)/shard_map/ppermute | solution.py:18
  89.3 6.5 %collective-permute-start.12 = (f32[2,80,16]{2,1,0:T(8,128)S(1)}, f32[2,80,16]{2,1,0:T(8,128)S(1)}, u32[]{:S(2)}, u32[]{:S(2)}) collective-permute-start(f32[2,80,16]{2,1,0:T(8,128)S(1)} %get-tuple-element.197), channel_id=1, source_target_pairs={{1,0},{2,1},{3,2},{4,3},{5,4},{6,5},{7,6},{8,7},{9,8},{10,9},{11,1... | collective-permute-start | bytes 30728 | tf_op jit(solution)/shard_map/ppermute | solution.py:18
  126.0 11.9 %all-gather = f32[8,80,16]{1,2,0:T(8,128)S(1)} all-gather(f32[2,80,16]{1,2,0:T(8,128)S(1)} %fusion.81), channel_id=2, replica_groups=mesh['dom'=128,'grp'=4] {'grp'}, dimensions={0}, use_global_device_ids=true | all-gather | bytes 51200 | tf_op jit(solution)/shard_map/all_gather | solution.py:112
  139.9 7.0 %collective-permute-start.17 = (f32[4,2,80,16]{2,1,3,0:T(2,128)S(1)}, f32[4,2,80,16]{2,1,3,0:T(2,128)S(1)}, u32[]{:S(2)}, u32[]{:S(2)}) collective-permute-start(f32[4,2,80,16]{2,1,3,0:T(2,128)S(1)} %get-tuple-element.229), channel_id=1, source_target_pairs={{4,0},{8,4},{12,8},{16,12},{20,16},{24,20},{28,24},{32,28},{36,32}... | collective-permute-start | bytes 122888 | tf_op jit(solution)/shard_map/ppermute | solution.py:18
  166.2 7.5 %collective-permute-start.19 = (f32[4,2,80,16]{2,1,3,0:T(2,128)S(1)}, f32[4,2,80,16]{2,1,3,0:T(2,128)S(1)}, u32[]{:S(2)}, u32[]{:S(2)}) collective-permute-start(f32[4,2,80,16]{2,1,3,0:T(2,128)S(1)} %divide_add_fusion.3), channel_id=1, source_target_pairs={{4,0},{8,4},{12,8},{16,12},{20,16},{24,20},{28,24},{32,28},{36,32}... | collective-permute-start | bytes 122888 | tf_op jit(solution)/shard_map/ppermute | solution.py:18
  192.6 7.0 %collective-permute-start.21 = (f32[4,2,80,16]{2,1,3,0:T(2,128)S(1)}, f32[4,2,80,16]{2,1,3,0:T(2,128)S(1)}, u32[]{:S(2)}, u32[]{:S(2)}) collective-permute-start(f32[4,2,80,16]{2,1,3,0:T(2,128)S(1)} %divide_add_fusion.2), channel_id=1, source_target_pairs={{4,0},{8,4},{12,8},{16,12},{20,16},{24,20},{28,24},{32,28},{36,32}... | collective-permute-start | bytes 122888 | tf_op jit(solution)/shard_map/ppermute | solution.py:18
  229.6 6.5 %collective-permute-start.26 = (f32[2,80,16]{2,1,0:T(8,128)S(1)}, f32[2,80,16]{2,1,0:T(8,128)S(1)}, u32[]{:S(2)}, u32[]{:S(2)}) collective-permute-start(f32[2,80,16]{2,1,0:T(8,128)S(1)} %get-tuple-element.187), channel_id=1, source_target_pairs={{1,0},{2,1},{3,2},{4,3},{5,4},{6,5},{7,6},{8,7},{9,8},{10,9},{11,1... | collective-permute-start | bytes 30728 | tf_op jit(solution)/shard_map/ppermute | solution.py:18
  236.1 5.0 collective-permute-start.27
  266.9 6.8 %collective-permute-start.34 = (f32[2,80,16]{2,1,0:T(8,128)S(1)}, f32[2,80,16]{2,1,0:T(8,128)S(1)}, u32[]{:S(2)}, u32[]{:S(2)}) collective-permute-start(f32[2,80,16]{2,1,0:T(8,128)S(1)} %get-tuple-element.177), channel_id=1, source_target_pairs={{1,0},{2,1},{3,2},{4,3},{5,4},{6,5},{7,6},{8,7},{9,8},{10,9},{11,1... | collective-permute-start | bytes 30728 | tf_op jit(solution)/shard_map/ppermute | solution.py:18
  295.5 4.9 collective-permute-start.39
  304.2 7.0 %collective-permute-start.42 = (f32[2,80,16]{2,1,0:T(8,128)S(1)}, f32[2,80,16]{2,1,0:T(8,128)S(1)}, u32[]{:S(2)}, u32[]{:S(2)}) collective-permute-start(f32[2,80,16]{2,1,0:T(8,128)S(1)} %get-tuple-element.167), channel_id=1, source_target_pairs={{1,0},{2,1},{3,2},{4,3},{5,4},{6,5},{7,6},{8,7},{9,8},{10,9},{11,1... | collective-permute-start | bytes 30728 | tf_op jit(solution)/shard_map/ppermute | solution.py:18
  341.6 7.2 %collective-permute-start.50 = (f32[2,80,16]{2,1,0:T(8,128)S(1)}, f32[2,80,16]{2,1,0:T(8,128)S(1)}, u32[]{:S(2)}, u32[]{:S(2)}) collective-permute-start(f32[2,80,16]{2,1,0:T(8,128)S(1)} %get-tuple-element.157), channel_id=1, source_target_pairs={{1,0},{2,1},{3,2},{4,3},{5,4},{6,5},{7,6},{8,7},{9,8},{10,9},{11,1... | collective-permute-start | bytes 30728 | tf_op jit(solution)/shard_map/ppermute | solution.py:18
  378.9 7.5 %collective-permute-start.58 = (f32[2,80,16]{2,1,0:T(8,128)S(1)}, f32[2,80,16]{2,1,0:T(8,128)S(1)}, u32[]{:S(2)}, u32[]{:S(2)}) collective-permute-start(f32[2,80,16]{2,1,0:T(8,128)S(1)} %get-tuple-element.147), channel_id=1, source_target_pairs={{1,0},{2,1},{3,2},{4,3},{5,4},{6,5},{7,6},{8,7},{9,8},{10,9},{11,1... | collective-permute-start | bytes 30728 | tf_op jit(solution)/shard_map/ppermute | solution.py:18
  403.8 12.2 %all-gather.1 = f32[8,80,16]{1,2,0:T(8,128)S(1)} all-gather(f32[2,80,16]{1,2,0:T(8,128)S(1)} %fusion.26), channel_id=3, replica_groups=mesh['dom'=128,'grp'=4] {'grp'}, dimensions={0}, use_global_device_ids=true | all-gather | bytes 51200 | tf_op jit(solution)/shard_map/all_gather | solution.py:112
  418.0 7.0 %collective-permute-start.63 = (f32[4,2,80,16]{2,1,3,0:T(2,128)S(1)}, f32[4,2,80,16]{2,1,3,0:T(2,128)S(1)}, u32[]{:S(2)}, u32[]{:S(2)}) collective-permute-start(f32[4,2,80,16]{2,1,3,0:T(2,128)S(1)} %get-tuple-element.215), channel_id=1, source_target_pairs={{4,0},{8,4},{12,8},{16,12},{20,16},{24,20},{28,24},{32,28},{36,32}... | collective-permute-start | bytes 122888 | tf_op jit(solution)/shard_map/ppermute | solution.py:18
  444.3 7.2 %collective-permute-start.65 = (f32[4,2,80,16]{2,1,3,0:T(2,128)S(1)}, f32[4,2,80,16]{2,1,3,0:T(2,128)S(1)}, u32[]{:S(2)}, u32[]{:S(2)}) collective-permute-start(f32[4,2,80,16]{2,1,3,0:T(2,128)S(1)} %divide_add_fusion.1), channel_id=1, source_target_pairs={{4,0},{8,4},{12,8},{16,12},{20,16},{24,20},{28,24},{32,28},{36,32}... | collective-permute-start | bytes 122888 | tf_op jit(solution)/shard_map/ppermute | solution.py:18
  470.7 7.0 %collective-permute-start.67 = (f32[4,2,80,16]{2,1,3,0:T(2,128)S(1)}, f32[4,2,80,16]{2,1,3,0:T(2,128)S(1)}, u32[]{:S(2)}, u32[]{:S(2)}) collective-permute-start(f32[4,2,80,16]{2,1,3,0:T(2,128)S(1)} %divide_add_fusion), channel_id=1, source_target_pairs={{4,0},{8,4},{12,8},{16,12},{20,16},{24,20},{28,24},{32,28},{36,32}... | collective-permute-start | bytes 122888 | tf_op jit(solution)/shard_map/ppermute | solution.py:18
  507.7 6.5 %collective-permute-start.72 = (f32[2,80,16]{2,1,0:T(8,128)S(1)}, f32[2,80,16]{2,1,0:T(8,128)S(1)}, u32[]{:S(2)}, u32[]{:S(2)}) collective-permute-start(f32[2,80,16]{2,1,0:T(8,128)S(1)} %get-tuple-element.137), channel_id=1, source_target_pairs={{1,0},{2,1},{3,2},{4,3},{5,4},{6,5},{7,6},{8,7},{9,8},{10,9},{11,1... | collective-permute-start | bytes 30728 | tf_op jit(solution)/shard_map/ppermute | solution.py:18
  514.3 5.0 collective-permute-start.73
  545.1 6.7 %collective-permute-start.80 = (f32[2,80,16]{2,1,0:T(8,128)S(1)}, f32[2,80,16]{2,1,0:T(8,128)S(1)}, u32[]{:S(2)}, u32[]{:S(2)}) collective-permute-start(f32[2,80,16]{2,1,0:T(8,128)S(1)} %get-tuple-element.127), channel_id=1, source_target_pairs={{1,0},{2,1},{3,2},{4,3},{5,4},{6,5},{7,6},{8,7},{9,8},{10,9},{11,1... | collective-permute-start | bytes 30728 | tf_op jit(solution)/shard_map/ppermute | solution.py:18
  (640 shorter events, 382.6 us)
Async XLA Ops:
  4.0 59.2 %collective-permute-start = (f32[2,80,16]{2,1,0:T(8,128)S(1)}, f32[2,80,16]{2,1,0:T(8,128)S(1)}, u32[]{:S(2)}, u32[]{:S(2)}) collective-permute-start(f32[2,80,16]{2,1,0:T(8,128)S(1)} %get-tuple-element.213), channel_id=1, source_target_pairs={{0,1},{1,2},{2,3},{3,4},{4,5},{5,6},{6,7},{7,8},{8,9},{9,10},{10,1... | collective-permute-start | bytes 30728 | tf_op jit(solution)/shard_map/ppermute | solution.py:18
  7.4 57.7 %collective-permute-start.1 = (f32[2,80,16]{2,1,0:T(8,128)S(1)}, f32[2,80,16]{2,1,0:T(8,128)S(1)}, u32[]{:S(2)}, u32[]{:S(2)}) collective-permute-start(f32[2,80,16]{2,1,0:T(8,128)S(1)} %get-tuple-element.212), channel_id=1, source_target_pairs={{0,2},{1,3},{2,4},{3,5},{4,6},{5,7},{6,8},{7,9},{8,10},{9,11},{10,... | collective-permute-start | bytes 30728 | tf_op jit(solution)/shard_map/ppermute | solution.py:18
  12.0 59.1 %collective-permute-start.2 = (f32[2,80,16]{2,1,0:T(8,128)S(1)}, f32[2,80,16]{2,1,0:T(8,128)S(1)}, u32[]{:S(2)}, u32[]{:S(2)}) collective-permute-start(f32[2,80,16]{2,1,0:T(8,128)S(1)} %get-tuple-element.211), channel_id=1, source_target_pairs={{0,3},{1,4},{2,5},{3,6},{4,7},{5,8},{6,9},{7,10},{8,11},{9,12},{10... | collective-permute-start | bytes 30728 | tf_op jit(solution)/shard_map/ppermute | solution.py:18
  14.5 59.1 %collective-permute-start.3 = (f32[2,80,16]{2,1,0:T(8,128)S(1)}, f32[2,80,16]{2,1,0:T(8,128)S(1)}, u32[]{:S(2)}, u32[]{:S(2)}) collective-permute-start(f32[2,80,16]{2,1,0:T(8,128)S(1)} %get-tuple-element.210), channel_id=1, source_target_pairs={{0,4},{1,5},{2,6},{3,7},{4,8},{5,9},{6,10},{7,11},{8,12},{9,13},{1... | collective-permute-start | bytes 30728 | tf_op jit(solution)/shard_map/ppermute | solution.py:18
  19.0 54.7 %collective-permute-start.4 = (f32[2,80,16]{2,1,0:T(8,128)S(1)}, f32[2,80,16]{2,1,0:T(8,128)S(1)}, u32[]{:S(2)}, u32[]{:S(2)}) collective-permute-start(f32[2,80,16]{2,1,0:T(8,128)S(1)} %get-tuple-element.209), channel_id=1, source_target_pairs={{1,0},{2,1},{3,2},{4,3},{5,4},{6,5},{7,6},{8,7},{9,8},{10,9},{11,1... | collective-permute-start | bytes 30728 | tf_op jit(solution)/shard_map/ppermute | solution.py:18
  82.5 19.4 %collective-permute-start.10 = (f32[2,80,16]{2,1,0:T(8,128)S(1)}, f32[2,80,16]{2,1,0:T(8,128)S(1)}, u32[]{:S(2)}, u32[]{:S(2)}) collective-permute-start(f32[2,80,16]{2,1,0:T(8,128)S(1)} %get-tuple-element.199), channel_id=1, source_target_pairs={{0,3},{1,4},{2,5},{3,6},{4,7},{5,8},{6,9},{7,10},{8,11},{9,12},{10... | collective-permute-start | bytes 30728 | tf_op jit(solution)/shard_map/ppermute | solution.py:18
  89.3 18.7 %collective-permute-start.12 = (f32[2,80,16]{2,1,0:T(8,128)S(1)}, f32[2,80,16]{2,1,0:T(8,128)S(1)}, u32[]{:S(2)}, u32[]{:S(2)}) collective-permute-start(f32[2,80,16]{2,1,0:T(8,128)S(1)} %get-tuple-element.197), channel_id=1, source_target_pairs={{1,0},{2,1},{3,2},{4,3},{5,4},{6,5},{7,6},{8,7},{9,8},{10,9},{11,1... | collective-permute-start | bytes 30728 | tf_op jit(solution)/shard_map/ppermute | solution.py:18
  221.1 20.0 %collective-permute-start.23 = (f32[2,80,16]{2,1,0:T(8,128)S(1)}, f32[2,80,16]{2,1,0:T(8,128)S(1)}, u32[]{:S(2)}, u32[]{:S(2)}) collective-permute-start(f32[2,80,16]{2,1,0:T(8,128)S(1)} %get-tuple-element.190), channel_id=1, source_target_pairs={{0,2},{1,3},{2,4},{3,5},{4,6},{5,7},{6,8},{7,9},{8,10},{9,11},{10,... | collective-permute-start | bytes 30728 | tf_op jit(solution)/shard_map/ppermute | solution.py:18
  227.6 19.0 %collective-permute-start.25 = (f32[2,80,16]{2,1,0:T(8,128)S(1)}, f32[2,80,16]{2,1,0:T(8,128)S(1)}, u32[]{:S(2)}, u32[]{:S(2)}) collective-permute-start(f32[2,80,16]{2,1,0:T(8,128)S(1)} %get-tuple-element.188), channel_id=1, source_target_pairs={{0,4},{1,5},{2,6},{3,7},{4,8},{5,9},{6,10},{7,11},{8,12},{9,13},{1... | collective-permute-start | bytes 30728 | tf_op jit(solution)/shard_map/ppermute | solution.py:18
  258.3 20.2 %collective-permute-start.31 = (f32[2,80,16]{2,1,0:T(8,128)S(1)}, f32[2,80,16]{2,1,0:T(8,128)S(1)}, u32[]{:S(2)}, u32[]{:S(2)}) collective-permute-start(f32[2,80,16]{2,1,0:T(8,128)S(1)} %get-tuple-element.180), channel_id=1, source_target_pairs={{0,2},{1,3},{2,4},{3,5},{4,6},{5,7},{6,8},{7,9},{8,10},{9,11},{10,... | collective-permute-start | bytes 30728 | tf_op jit(solution)/shard_map/ppermute | solution.py:18
  265.0 18.6 %collective-permute-start.33 = (f32[2,80,16]{2,1,0:T(8,128)S(1)}, f32[2,80,16]{2,1,0:T(8,128)S(1)}, u32[]{:S(2)}, u32[]{:S(2)}) collective-permute-start(f32[2,80,16]{2,1,0:T(8,128)S(1)} %get-tuple-element.178), channel_id=1, source_target_pairs={{0,4},{1,5},{2,6},{3,7},{4,8},{5,9},{6,10},{7,11},{8,12},{9,13},{1... | collective-permute-start | bytes 30728 | tf_op jit(solution)/shard_map/ppermute | solution.py:18
  292.9 18.4 %collective-permute-start.38 = (f32[2,80,16]{2,1,0:T(8,128)S(1)}, f32[2,80,16]{2,1,0:T(8,128)S(1)}, u32[]{:S(2)}, u32[]{:S(2)}) collective-permute-start(f32[2,80,16]{2,1,0:T(8,128)S(1)} %get-tuple-element.171), channel_id=1, source_target_pairs={{0,1},{1,2},{2,3},{3,4},{4,5},{5,6},{6,7},{7,8},{8,9},{9,10},{10,1... | collective-permute-start | bytes 30728 | tf_op jit(solution)/shard_map/ppermute | solution.py:18
  295.5 20.3 %collective-permute-start.39 = (f32[2,80,16]{2,1,0:T(8,128)S(1)}, f32[2,80,16]{2,1,0:T(8,128)S(1)}, u32[]{:S(2)}, u32[]{:S(2)}) collective-permute-start(f32[2,80,16]{2,1,0:T(8,128)S(1)} %get-tuple-element.170), channel_id=1, source_target_pairs={{0,2},{1,3},{2,4},{3,5},{4,6},{5,7},{6,8},{7,9},{8,10},{9,11},{10,... | collective-permute-start | bytes 30728 | tf_op jit(solution)/shard_map/ppermute | solution.py:18
  302.3 18.5 %collective-permute-start.41 = (f32[2,80,16]{2,1,0:T(8,128)S(1)}, f32[2,80,16]{2,1,0:T(8,128)S(1)}, u32[]{:S(2)}, u32[]{:S(2)}) collective-permute-start(f32[2,80,16]{2,1,0:T(8,128)S(1)} %get-tuple-element.168), channel_id=1, source_target_pairs={{0,4},{1,5},{2,6},{3,7},{4,8},{5,9},{6,10},{7,11},{8,12},{9,13},{1... | collective-permute-start | bytes 30728 | tf_op jit(solution)/shard_map/ppermute | solution.py:18
  330.2 18.6 %collective-permute-start.46 = (f32[2,80,16]{2,1,0:T(8,128)S(1)}, f32[2,80,16]{2,1,0:T(8,128)S(1)}, u32[]{:S(2)}, u32[]{:S(2)}) collective-permute-start(f32[2,80,16]{2,1,0:T(8,128)S(1)} %get-tuple-element.161), channel_id=1, source_target_pairs={{0,1},{1,2},{2,3},{3,4},{4,5},{5,6},{6,7},{7,8},{8,9},{9,10},{10,1... | collective-permute-start | bytes 30728 | tf_op jit(solution)/shard_map/ppermute | solution.py:18
  333.1 20.1 %collective-permute-start.47 = (f32[2,80,16]{2,1,0:T(8,128)S(1)}, f32[2,80,16]{2,1,0:T(8,128)S(1)}, u32[]{:S(2)}, u32[]{:S(2)}) collective-permute-start(f32[2,80,16]{2,1,0:T(8,128)S(1)} %get-tuple-element.160), channel_id=1, source_target_pairs={{0,2},{1,3},{2,4},{3,5},{4,6},{5,7},{6,8},{7,9},{8,10},{9,11},{10,... | collective-permute-start | bytes 30728 | tf_op jit(solution)/shard_map/ppermute | solution.py:18
  339.6 18.4 %collective-permute-start.49 = (f32[2,80,16]{2,1,0:T(8,128)S(1)}, f32[2,80,16]{2,1,0:T(8,128)S(1)}, u32[]{:S(2)}, u32[]{:S(2)}) collective-permute-start(f32[2,80,16]{2,1,0:T(8,128)S(1)} %get-tuple-element.158), channel_id=1, source_target_pairs={{0,4},{1,5},{2,6},{3,7},{4,8},{5,9},{6,10},{7,11},{8,12},{9,13},{1... | collective-permute-start | bytes 30728 | tf_op jit(solution)/shard_map/ppermute | solution.py:18
  367.5 18.9 %collective-permute-start.54 = (f32[2,80,16]{2,1,0:T(8,128)S(1)}, f32[2,80,16]{2,1,0:T(8,128)S(1)}, u32[]{:S(2)}, u32[]{:S(2)}) collective-permute-start(f32[2,80,16]{2,1,0:T(8,128)S(1)} %get-tuple-element.151), channel_id=1, source_target_pairs={{0,1},{1,2},{2,3},{3,4},{4,5},{5,6},{6,7},{7,8},{8,9},{9,10},{10,1... | collective-permute-start | bytes 30728 | tf_op jit(solution)/shard_map/ppermute | solution.py:18
  370.6 19.8 %collective-permute-start.55 = (f32[2,80,16]{2,1,0:T(8,128)S(1)}, f32[2,80,16]{2,1,0:T(8,128)S(1)}, u32[]{:S(2)}, u32[]{:S(2)}) collective-permute-start(f32[2,80,16]{2,1,0:T(8,128)S(1)} %get-tuple-element.150), channel_id=1, source_target_pairs={{0,2},{1,3},{2,4},{3,5},{4,6},{5,7},{6,8},{7,9},{8,10},{9,11},{10,... | collective-permute-start | bytes 30728 | tf_op jit(solution)/shard_map/ppermute | solution.py:18
  377.0 18.4 %collective-permute-start.57 = (f32[2,80,16]{2,1,0:T(8,128)S(1)}, f32[2,80,16]{2,1,0:T(8,128)S(1)}, u32[]{:S(2)}, u32[]{:S(2)}) collective-permute-start(f32[2,80,16]{2,1,0:T(8,128)S(1)} %get-tuple-element.148), channel_id=1, source_target_pairs={{0,4},{1,5},{2,6},{3,7},{4,8},{5,9},{6,10},{7,11},{8,12},{9,13},{1... | collective-permute-start | bytes 30728 | tf_op jit(solution)/shard_map/ppermute | solution.py:18
  499.3 20.0 %collective-permute-start.69 = (f32[2,80,16]{2,1,0:T(8,128)S(1)}, f32[2,80,16]{2,1,0:T(8,128)S(1)}, u32[]{:S(2)}, u32[]{:S(2)}) collective-permute-start(f32[2,80,16]{2,1,0:T(8,128)S(1)} %get-tuple-element.140), channel_id=1, source_target_pairs={{0,2},{1,3},{2,4},{3,5},{4,6},{5,7},{6,8},{7,9},{8,10},{9,11},{10,... | collective-permute-start | bytes 30728 | tf_op jit(solution)/shard_map/ppermute | solution.py:18
  505.8 19.0 %collective-permute-start.71 = (f32[2,80,16]{2,1,0:T(8,128)S(1)}, f32[2,80,16]{2,1,0:T(8,128)S(1)}, u32[]{:S(2)}, u32[]{:S(2)}) collective-permute-start(f32[2,80,16]{2,1,0:T(8,128)S(1)} %get-tuple-element.138), channel_id=1, source_target_pairs={{0,4},{1,5},{2,6},{3,7},{4,8},{5,9},{6,10},{7,11},{8,12},{9,13},{1... | collective-permute-start | bytes 30728 | tf_op jit(solution)/shard_map/ppermute | solution.py:18
  536.5 20.2 %collective-permute-start.77 = (f32[2,80,16]{2,1,0:T(8,128)S(1)}, f32[2,80,16]{2,1,0:T(8,128)S(1)}, u32[]{:S(2)}, u32[]{:S(2)}) collective-permute-start(f32[2,80,16]{2,1,0:T(8,128)S(1)} %get-tuple-element.130), channel_id=1, source_target_pairs={{0,2},{1,3},{2,4},{3,5},{4,6},{5,7},{6,8},{7,9},{8,10},{9,11},{10,... | collective-permute-start | bytes 30728 | tf_op jit(solution)/shard_map/ppermute | solution.py:18
  543.1 18.6 %collective-permute-start.79 = (f32[2,80,16]{2,1,0:T(8,128)S(1)}, f32[2,80,16]{2,1,0:T(8,128)S(1)}, u32[]{:S(2)}, u32[]{:S(2)}) collective-permute-start(f32[2,80,16]{2,1,0:T(8,128)S(1)} %get-tuple-element.128), channel_id=1, source_target_pairs={{0,4},{1,5},{2,6},{3,7},{4,8},{5,9},{6,10},{7,11},{8,12},{9,13},{1... | collective-permute-start | bytes 30728 | tf_op jit(solution)/shard_map/ppermute | solution.py:18
  (70 other events, 724.9 us)
where the time goes:
time: 580 us; the launch traced here: 571 us
  starting transfers between devices  310 us (53%)
  local copies, waits for them, and re-layouts  152 us (26%)
  blocking collectives  60.2 us (10%)
  waiting for transfers between devices  35 us (6%)
  other arithmetic  8.77 us (2%)
    ppermute x84, starting transfers between devices, from_behind(): return lax.ppermute(block, axis, route)  310 us
    gather x252, local copies, waits for them, and re-layouts, apply_rows(): jnp.take(extended, neighbours[branch], axis=2)  129 us
    ppermute x84, waiting for transfers between devices, from_behind(): return lax.ppermute(block, axis, route)  35 us
    all_gather x2, blocking collectives, body(): lax.all_gather(coarse_source[None], 'grp', axis=0, tiled=True)  24.1 us
    all_gather x1, blocking collectives, body(): lax.all_gather(coarse_horizontal, 'grp', axis=0, tiled=True)  12.2 us
    all_gather x1, blocking collectives, body(): lax.all_gather(coarse_neighbours, 'grp', axis=0, tiled=True)  12.1 us
    all_gather x1, blocking collectives, body(): lax.all_gather(coarse_vertical, 'grp', axis=0, tiled=True)  11.9 us
  transfers between devices with their start and end apart: 84, of which 16 were waited for; matrix products, arithmetic and copies ran while one was open for 0% of the time, Pallas kernels for 0%

commit v1 on v0

v1 whole, which is shorter than its diff:
```python
import functools

import jax
import jax.numpy as jnp
from jax import lax
from jax.experimental import pallas as pl
from jax.experimental.pallas import tpu as pltpu
from jax.sharding import PartitionSpec as P

CYCLES = 2
PRE = 2
POST = 2
CSWEEPS = 4

OMEGA = 0.8
HIGHEST = lax.Precision.HIGHEST
MESH = pl.DeviceIdType.MESH
LANES = 128


def mm(a, b):
    return jnp.dot(a, b, precision=HIGHEST, preferred_element_type=jnp.float32)


def vcycle_kernel(
    n_parts,
    n_grp,
    reach,
    width,
    rhs_ref,
    diag_ref,
    v0_ref,
    v1_ref,
    h_ref,
    w_ref,
    mt_ref,
    st_ref,
    at_ref,
    a_ref,
    mct_ref,
    cdiag_ref,
    cv0_ref,
    cv1_ref,
    ch_ref,
    out_ref,
    ext,
    sendbuf,
    cext,
    send_sem,
    recv_sem,
    csend_sem,
    crecv_sem,
):
    me = lax.axis_index("dom") * n_grp + lax.axis_index("grp")
    offsets = list(range(1, reach + 1)) + [-d for d in range(1, reach + 1)]
    columns = mt_ref.shape[1] // 2
    c1 = cdiag_ref.shape[0]
    n_slots = len(offsets)

    def valid(q):
        return jnp.logical_and(q >= 0, q < n_parts)

    def device(q):
        return (lax.div(q, n_grp), lax.rem(q, n_grp))

    ext[...] = jnp.zeros_like(ext)
    cext[...] = jnp.zeros_like(cext)

    barrier = pltpu.get_barrier_semaphore()
    for d in offsets:
        @pl.when(valid(me + d))
        def _():
            pl.semaphore_signal(barrier, 1, device_id=device(me + d), device_id_type=MESH)
    peers = sum(valid(me + d).astype(jnp.int32) for d in offsets)
    pl.semaphore_wait(barrier, peers)

    lane = lax.broadcasted_iota(jnp.int32, (8, LANES), 1)
    probe = pltpu.roll(lane, 1, 1)
    expected = jnp.where(lane == 0, LANES - 1, lane - 1)
    forward = (probe == expected)[0:1, :]

    def shifted(x):
        a = pltpu.roll(x, 1, 1)
        b = pltpu.roll(x, LANES - 1, 1)
        lower = jnp.where(forward, a, b)
        upper = jnp.where(forward, b, a)
        return lower, upper

    diag = diag_ref[...]
    v0 = v0_ref[...]
    v1 = v1_ref[...]
    w = w_ref[...]
    cdiag = cdiag_ref[...]
    cv0 = cv0_ref[...]
    cv1 = cv1_ref[...]
    rhs = rhs_ref[...]

    def halves(x):
        return [x[:, t * LANES:(t + 1) * LANES] for t in range(x.shape[1] // LANES)]

    def fine_copy(slot, s):
        rows = pl.ds(s * width, width)
        return pltpu.make_async_remote_copy(
            src_ref=sendbuf.at[rows],
            dst_ref=ext.at[slot, pl.ds(columns + s * width, width)],
            send_sem=send_sem.at[s],
            recv_sem=recv_sem.at[slot, s],
            device_id=device(me + offsets[s]),
            device_id_type=MESH,
        )

    fine_round = [0]

    def fine_apply(field):
        slot = fine_round[0] % 2
        fine_round[0] += 1
        sendbuf[...] = mm(st_ref[...], field)
        for s in range(n_slots):
            @pl.when(valid(me + offsets[s]))
            def _():
                fine_copy(slot, s).start()
        ext[slot, pl.ds(0, columns), :] = field
        for s in range(n_slots):
            @pl.when(valid(me + offsets[s]))
            def _():
                fine_copy(slot, s).wait_send()

            @pl.when(valid(me - offsets[s]))
            def _():
                fine_copy(slot, s).wait_recv()
        gathered = mm(mt_ref[...], ext[slot])
        totals = []
        for t, part in enumerate(halves(field)):
            lower, upper = shifted(part)
            total = diag * part + v0 * lower + v1 * upper
            for n in range(h_ref.shape[0]):
                total = total + h_ref[n] * gathered[n * columns:(n + 1) * columns, t * LANES:(t + 1) * LANES]
            totals.append(total)
        return jnp.concatenate(totals, 1)

    def coarse_copy(slot, k):
        d = offsets[k]
        return pltpu.make_async_remote_copy(
            src_ref=cext.at[slot, pl.ds(reach * c1, c1)],
            dst_ref=cext.at[slot, pl.ds((reach - d) * c1, c1)],
            send_sem=csend_sem.at[k],
            recv_sem=crecv_sem.at[slot, k],
            device_id=device(me + d),
            device_id_type=MESH,
        )

    coarse_round = [0]

    def coarse_apply(corr):
        slot = coarse_round[0] % 2
        coarse_round[0] += 1
        cext[slot, pl.ds(reach * c1, c1), :] = corr
        for k in range(n_slots):
            @pl.when(valid(me + offsets[k]))
            def _():
                coarse_copy(slot, k).start()
        for k in range(n_slots):
            @pl.when(valid(me + offsets[k]))
            def _():
                coarse_copy(slot, k).wait_send()

            @pl.when(valid(me - offsets[k]))
            def _():
                coarse_copy(slot, k).wait_recv()
        gathered = mm(mct_ref[...], cext[slot])
        totals = []
        for t, part in enumerate(halves(corr)):
            lower, upper = shifted(part)
            total = cdiag * part + cv0 * lower + cv1 * upper
            for n in range(ch_ref.shape[0]):
                total = total + ch_ref[n] * gathered[n * c1:(n + 1) * c1, t * LANES:(t + 1) * LANES]
            totals.append(total)
        return jnp.concatenate(totals, 1)

    def per_half(x, coeff, op):
        return jnp.concatenate([op(part, coeff) for part in halves(x)], 1)

    solution = per_half(OMEGA * rhs, diag, lambda x, c: x / c)
    for cycle_index in range(CYCLES):
        for sweep_index in range(PRE):
            if cycle_index == 0 and sweep_index == 0:
                continue
            step = OMEGA * (rhs - fine_apply(solution))
            solution = solution + per_half(step, diag, lambda x, c: x / c)
        residual = rhs - fine_apply(solution)
        weighted = per_half(residual, w, lambda x, c: x * c)
        coarse_source = mm(at_ref[...], weighted)
        correction = per_half(OMEGA * coarse_source, cdiag, lambda x, c: x / c)
        for coarse_sweep_index in range(CSWEEPS - 1):
            step = OMEGA * (coarse_source - coarse_apply(correction))
            correction = correction + per_half(step, cdiag, lambda x, c: x / c)
        lifted = mm(a_ref[...], correction)
        solution = solution + per_half(lifted, w, lambda x, c: x * c)
        for sweep_index in range(POST):
            step = OMEGA * (rhs - fine_apply(solution))
            solution = solution + per_half(step, diag, lambda x, c: x / c)
    out_ref[...] = solution


def to_lanes(x, fill=0.0):
    layers = x.shape[-2]
    moved = jnp.moveaxis(x, -1, 0)
    pad = [(0, 0)] * (moved.ndim - 1) + [(0, LANES - layers)]
    padded = jnp.pad(moved, pad, constant_values=fill)
    return padded.reshape(padded.shape[0], -1)


def body(
    right_side,
    absorption,
    vertical,
    horizontal,
    neighbours,
    send_index,
    aggregate,
    weights,
    coarse_vertical,
    coarse_horizontal,
    coarse_neighbours,
    *,
    n_parts,
    n_grp,
):
    rhs = right_side[0]
    vertical_rows = vertical[0]
    horizontal_rows = horizontal[0]
    tracers, layers, columns = rhs.shape
    diagonal = (
        absorption[0]
        + jnp.abs(vertical_rows[0])
        + jnp.abs(vertical_rows[1])
        + jnp.sum(jnp.abs(horizontal_rows), axis=0)
    )
    cvert = coarse_vertical[0]
    chor = coarse_horizontal[0]
    coarse_diagonal = (
        0.5 + jnp.abs(cvert[0]) + jnp.abs(cvert[1]) + jnp.sum(jnp.abs(chor), axis=0)
    )
    layer = lax.broadcasted_iota(jnp.int32, (layers, 1), 0)
    v0 = jnp.where(layer == 0, 0.0, vertical_rows[0])
    v1 = jnp.where(layer == layers - 1, 0.0, vertical_rows[1])
    cv0 = jnp.where(layer == 0, 0.0, cvert[0])
    cv1 = jnp.where(layer == layers - 1, 0.0, cvert[1])

    reach = send_index.shape[1] // 2
    width = send_index.shape[2]
    c1 = coarse_neighbours.shape[2]
    nb = neighbours[0]
    n_nb = nb.shape[0]
    ext_rows = columns + 2 * reach * width
    mt = (nb.reshape(-1)[:, None] == jnp.arange(ext_rows, dtype=jnp.int32)[None, :]).astype(jnp.float32)
    st = (send_index[0].reshape(-1)[:, None] == jnp.arange(columns, dtype=jnp.int32)[None, :]).astype(jnp.float32)
    at = (aggregate[0][None, :] == jnp.arange(c1, dtype=jnp.int32)[:, None]).astype(jnp.float32)
    a = at.T
    coarse_rows = (2 * reach + 1) * c1
    mct = (coarse_neighbours[0].reshape(-1)[:, None] == jnp.arange(coarse_rows, dtype=jnp.int32)[None, :]).astype(jnp.float32)

    args = (
        to_lanes(rhs),
        to_lanes(diagonal, 1.0),
        to_lanes(v0),
        to_lanes(v1),
        jnp.stack([to_lanes(horizontal_rows[n]) for n in range(horizontal_rows.shape[0])]),
        to_lanes(weights[0]),
        mt,
        st,
        at,
        a,
        mct,
        to_lanes(coarse_diagonal, 1.0),
        to_lanes(cv0),
        to_lanes(cv1),
        jnp.stack([to_lanes(chor[n]) for n in range(chor.shape[0])]),
    )
    n_slots = 2 * reach
    out = pl.pallas_call(
        functools.partial(vcycle_kernel, n_parts, n_grp, reach, width),
        out_shape=jax.ShapeDtypeStruct((columns, tracers * LANES), jnp.float32),
        in_specs=[pl.BlockSpec(memory_space=pltpu.VMEM)] * len(args),
        out_specs=pl.BlockSpec(memory_space=pltpu.VMEM),
        scratch_shapes=[
            pltpu.VMEM((2, ext_rows, tracers * LANES), jnp.float32),
            pltpu.VMEM((n_slots * width, tracers * LANES), jnp.float32),
            pltpu.VMEM((2, coarse_rows, tracers * LANES), jnp.float32),
            pltpu.SemaphoreType.DMA((n_slots,)),
            pltpu.SemaphoreType.DMA((2, n_slots)),
            pltpu.SemaphoreType.DMA((n_slots,)),
            pltpu.SemaphoreType.DMA((2, n_slots)),
        ],
        compiler_params=pltpu.CompilerParams(collective_id=0, has_side_effects=True),
    )(*args)
    result = out.reshape(columns, tracers, LANES)[:, :, :layers]
    return jnp.transpose(result, (1, 2, 0))[None]


def solution(mesh):
    placed = (
        P(("dom", "grp"), None, None, None),
        P(("dom", "grp"), None, None),
        P(("dom", "grp"), None, None, None),
        P(("dom", "grp"), None, None, None),
        P(("dom", "grp"), None, None),
        P(("dom", "grp"), None, None),
        P(("dom", "grp"), None),
        P(("dom", "grp"), None, None),
        P(("dom", "grp"), None, None, None),
        P(("dom", "grp"), None, None, None),
        P(("dom", "grp"), None, None),
    )
    n_grp = mesh.shape["grp"]
    n_parts = mesh.shape["dom"] * n_grp
    return jax.shard_map(
        functools.partial(body, n_parts=n_parts, n_grp=n_grp),
        mesh=mesh,
        in_specs=placed,
        out_specs=P(("dom", "grp"), None, None, None),
        check_vma=False,
    )
```

time: 580 us -> 129 us (0.22); the launches traced: 571 us -> 128 us
  starting transfers between devices: 310 us -> 0 us
  local copies, waits for them, and re-layouts: 152 us -> 12 us
  Pallas kernels: 0 us -> 110 us
  blocking collectives: 60.2 us -> 0 us
  waiting for transfers between devices: 35 us -> 0 us
    ppermute x84 -> x0, starting transfers between devices: 310 us -> none  [from_behind(): return lax.ppermute(block, axis, route)]
    gather x270 -> x0, local copies, waits for them, and re-layouts: 137 us -> none  [the longest x252 129 us: apply_rows(): jnp.take(extended, neighbours[branch], axis=2)]
    pallas_call x0 -> x1, Pallas kernels: none -> 110 us  [body(): pl.pallas_call(functools.partial(vcycle_kernel, n_parts, n_grp, reach, wi...]
    all_gather x5 -> x0, blocking collectives: 60.2 us -> none  [the longest x2 24.1 us: body(): lax.all_gather(coarse_source[None], 'grp', axis=0, tiled=True)]
    ppermute x84 -> x0, waiting for transfers between devices: 35 us -> none  [from_behind(): return lax.ppermute(block, axis, route)]
  transfers between devices with their start and end apart: 84 -> 0, of which waited for: 16 -> 0; matrix products, arithmetic and copies ran while one was open for 0% -> 0% of each run, Pallas kernels for 0% -> 0%
where the time goes in v1:
time: 129 us; the launch traced here: 128 us
  Pallas kernels  110 us (85%)
  local copies, waits for them, and re-layouts  12 us (9%)
  other arithmetic  5.65 us (4%)
    pallas_call x1, Pallas kernels, body(): pl.pallas_call(functools.partial(vcycle_kernel, n_parts, n_grp, reach, wi...  110 us
    unnamed x44, local copies, waits for them, and re-layouts  4.35 us
    pad x8, local copies, waits for them, and re-layouts, to_lanes(): padded = jnp.pad(moved, pad, constant_values=fill)  4.33 us

profile of v1, /device:TPU:32, one launch (start us, length us, event | category | flops | bytes accessed | tf_op | source)
XLA Modules:
  0.0 128.4 jit_solution(16014178242140157916)
XLA Ops:
  0.0 0.8 eq.95
  0.8 0.7 copy-done.9
  1.5 0.7 copy-done.10
  2.2 0.6 copy-done.11
  2.8 0.6 fusion.16.at_ref
  3.4 0.8 abs_reduce_fusion.1
  4.3 0.6 pad.76.cv1_ref
  4.9 0.6 pad.74.cdiag_ref
  5.5 0.6 pad.75.cv0_ref
  6.1 1.0 abs_reduce_fusion
  7.1 0.7 copy-done.2
  7.9 0.7 fusion.8.st_ref
  8.8 0.7 fusion.9.a_ref
  9.7 0.6 pad.73.w_ref
  10.3 0.3 copy-done.3
  10.8 0.6 pad.66.v1_ref
  11.4 0.6 pad.64.diag_ref
  12.1 0.6 pad.65.v0_ref
  12.7 0.7 fusion.1.mct_ref
  13.6 0.8 copy.37.rhs_ref
  15.3 1.1 fusion.mt_ref
  16.3 110.4 %shard_map.109 = f32[128,256]{1,0:T(8,128)} custom-call(f32[128,256]{1,0:T(8,128)} %copy.37.rhs_ref, f32[128,128]{1,0:T(8,128)} %pad.64.diag_ref, f32[128,128]{1,0:T(8,128)} %pad.65.v0_ref, f32[128,128]{1,0:T(8,128)} %pad.66.v1_ref, f32[6,128,128]{2,1,0:T(8,128)} %copy-done.1, f32[128,128]{1,0:T(8,128)} %pad.73.w_ref, f32[768,256]{1,0:T(8,128)} %fusion.mt_ref, ...), custom_call_target="tpu_custom_call" | custom-call | tf_op jit(solution)/shard_map/pallas_call | solution.py:281
  126.8 1.0 copy.38
  127.8 0.6 slice_bitcast_fusion
  (52 shorter events, 1.8 us)
Async XLA Ops:
  0.8 0.7 copy-start.9
  1.5 0.7 copy-start.10
  2.2 0.7 copy-start.11
  3.4 0.8 copy-start.8
  7.0 0.8 copy-start.2
  7.9 0.8 copy-start.6
  7.9 0.9 copy-start.5
  8.8 0.8 copy-start.7
  9.7 0.9 copy-start.3
  12.7 0.9 copy-start.4
  13.6 0.9 copy-start
  15.3 1.1 copy-start.1

commit v2 on v1

v2 whole, which is shorter than its diff:
```python
import functools

import jax
import jax.numpy as jnp
from jax import lax
from jax.experimental import pallas as pl
from jax.experimental.pallas import tpu as pltpu
from jax.sharding import PartitionSpec as P

CYCLES = 2
PRE = 2
POST = 2
CSWEEPS = 4

OMEGA = 0.8
HIGHEST = lax.Precision.HIGHEST
MESH = pl.DeviceIdType.MESH
LANES = 128
F32 = jnp.float32


def mm(a, b):
    return jnp.dot(a, b, precision=HIGHEST, preferred_element_type=F32)


def vcycle_kernel(
    n_parts,
    n_grp,
    reach,
    width,
    rhs_hbm,
    absorption_hbm,
    vertical_hbm,
    horizontal_hbm,
    weights_hbm,
    nb_hbm,
    si_hbm,
    agg_hbm,
    cnb_hbm,
    cprep_hbm,
    out_hbm,
    rhs_v,
    absorption_v,
    vertical_v,
    horizontal_v,
    weights_v,
    nb_v,
    si_v,
    agg_v,
    cnb_v,
    cprep_v,
    out_v,
    load_sem,
    mt_s,
    ghost,
    sendbuf,
    cext,
    send_sem,
    recv_sem,
    csend_sem,
    crecv_sem,
):
    me = lax.axis_index("dom") * n_grp + lax.axis_index("grp")
    offsets = list(range(1, reach + 1)) + [-d for d in range(1, reach + 1)]
    n_slots = len(offsets)
    tracers, layers, columns = rhs_v.shape[1:]
    n_nb = nb_v.shape[0]
    c1 = cprep_v.shape[1]
    n_ch = cprep_v.shape[0] - 3
    halo = n_slots * width

    def valid(q):
        return jnp.logical_and(q >= 0, q < n_parts)

    def device(q):
        return (lax.div(q, n_grp), lax.rem(q, n_grp))

    loads = [
        pltpu.make_async_copy(src, dst, load_sem.at[i])
        for i, (src, dst) in enumerate(
            [
                (rhs_hbm, rhs_v),
                (absorption_hbm, absorption_v),
                (vertical_hbm, vertical_v),
                (horizontal_hbm, horizontal_v),
                (weights_hbm, weights_v),
                (nb_hbm, nb_v),
                (si_hbm, si_v),
                (agg_hbm, agg_v),
                (cnb_hbm, cnb_v),
                (cprep_hbm, cprep_v),
            ]
        )
    ]
    for copy in loads:
        copy.start()

    ghost[...] = jnp.zeros_like(ghost)
    cext[...] = jnp.zeros_like(cext)

    barrier = pltpu.get_barrier_semaphore()
    for d in offsets:
        @pl.when(valid(me + d))
        def _():
            pl.semaphore_signal(barrier, 1, device_id=device(me + d), device_id_type=MESH)
    peers = sum(valid(me + d).astype(jnp.int32) for d in offsets)
    pl.semaphore_wait(barrier, peers)

    for copy in loads:
        copy.wait()

    lane = lax.broadcasted_iota(jnp.int32, (8, LANES), 1)
    probe = pltpu.roll(lane, 1, 1)
    expected = jnp.where(lane == 0, LANES - 1, lane - 1)
    forward = (probe == expected)[0:1, :]
    layer_lane = lax.broadcasted_iota(jnp.int32, (1, LANES), 1)
    live = layer_lane < layers

    def shifted(x):
        a = pltpu.roll(x, 1, 1)
        b = pltpu.roll(x, LANES - 1, 1)
        lower = jnp.where(forward, a, b)
        upper = jnp.where(forward, b, a)
        return lower, upper

    pad_rows = jnp.zeros((LANES - layers, columns), F32)

    def to_cols(slab):
        return jnp.transpose(jnp.concatenate([slab, pad_rows], 0))

    ab = absorption_v[0]
    vr0 = vertical_v[0, 0]
    vr1 = vertical_v[0, 1]
    diag_rows = ab + jnp.abs(vr0) + jnp.abs(vr1)
    hsum = jnp.abs(horizontal_v[0, 0])
    for n in range(1, horizontal_v.shape[1]):
        hsum = hsum + jnp.abs(horizontal_v[0, n])
    diag_rows = diag_rows + hsum
    diag = jnp.where(live, to_cols(diag_rows), 1.0)
    v0 = jnp.where(layer_lane == 0, 0.0, to_cols(vr0))
    v1 = jnp.where(layer_lane == layers - 1, 0.0, to_cols(vr1))
    h = [to_cols(horizontal_v[0, n]) for n in range(horizontal_v.shape[1])]
    w = to_cols(weights_v[0])
    rhs = jnp.concatenate([to_cols(rhs_v[0, t]) for t in range(tracers)], 1)

    ext_rows = columns + halo
    k_iota = lax.broadcasted_iota(jnp.int32, (ext_rows, columns), 0)
    for n in range(n_nb):
        chosen = (k_iota == nb_v[n:n + 1, :]).astype(F32)
        mt_s[pl.ds(n * columns, columns), :] = jnp.transpose(chosen)
    st = jnp.transpose((lax.broadcasted_iota(jnp.int32, (columns, halo), 0) == si_v[...]).astype(F32))
    at = (lax.broadcasted_iota(jnp.int32, (c1, columns), 0) == agg_v[...]).astype(F32)
    a_full = jnp.transpose((lax.broadcasted_iota(jnp.int32, (LANES, columns), 0) == agg_v[...]).astype(F32))
    a = a_full[:, :c1]
    coarse_rows = cext.shape[1]
    n_crow = n_ch * c1
    mct = jnp.transpose(
        (lax.broadcasted_iota(jnp.int32, (coarse_rows, cnb_v.shape[1]), 0) == cnb_v[...]).astype(F32)
    )[:n_crow]

    cdiag = cprep_v[0]
    cv0 = cprep_v[1]
    cv1 = cprep_v[2]

    def halves(x):
        return [x[:, t * LANES:(t + 1) * LANES] for t in range(x.shape[1] // LANES)]

    def fine_copy(slot, s):
        rows = pl.ds(s * width, width)
        return pltpu.make_async_remote_copy(
            src_ref=sendbuf.at[rows],
            dst_ref=ghost.at[slot, rows],
            send_sem=send_sem.at[s],
            recv_sem=recv_sem.at[slot, s],
            device_id=device(me + offsets[s]),
            device_id_type=MESH,
        )

    fine_round = [0]

    def fine_apply(field):
        slot = fine_round[0] % 2
        fine_round[0] += 1
        sendbuf[...] = mm(st, field)
        for s in range(n_slots):
            @pl.when(valid(me + offsets[s]))
            def _():
                fine_copy(slot, s).start()
        local = mm(mt_s[:, pl.ds(0, columns)], field)
        bases = []
        for part in halves(field):
            lower, upper = shifted(part)
            bases.append(diag * part + v0 * lower + v1 * upper)
        for s in range(n_slots):
            @pl.when(valid(me + offsets[s]))
            def _():
                fine_copy(slot, s).wait_send()

            @pl.when(valid(me - offsets[s]))
            def _():
                fine_copy(slot, s).wait_recv()
        gathered = local + mm(mt_s[:, pl.ds(columns, halo)], ghost[slot])
        totals = []
        for t, total in enumerate(bases):
            for n in range(n_nb):
                total = total + h[n] * gathered[n * columns:(n + 1) * columns, t * LANES:(t + 1) * LANES]
            totals.append(total)
        return jnp.concatenate(totals, 1)

    def coarse_copy(slot, k):
        d = offsets[k]
        return pltpu.make_async_remote_copy(
            src_ref=cext.at[slot, pl.ds(reach * c1, c1)],
            dst_ref=cext.at[slot, pl.ds((reach - d) * c1, c1)],
            send_sem=csend_sem.at[k],
            recv_sem=crecv_sem.at[slot, k],
            device_id=device(me + d),
            device_id_type=MESH,
        )

    coarse_round = [0]

    def coarse_apply(corr):
        slot = coarse_round[0] % 2
        coarse_round[0] += 1
        cext[slot, pl.ds(reach * c1, c1), :] = corr
        for k in range(n_slots):
            @pl.when(valid(me + offsets[k]))
            def _():
                coarse_copy(slot, k).start()
        bases = []
        for part in halves(corr):
            lower, upper = shifted(part)
            bases.append(cdiag * part + cv0 * lower + cv1 * upper)
        for k in range(n_slots):
            @pl.when(valid(me + offsets[k]))
            def _():
                coarse_copy(slot, k).wait_send()

            @pl.when(valid(me - offsets[k]))
            def _():
                coarse_copy(slot, k).wait_recv()
        gathered = mm(mct, cext[slot])
        totals = []
        for t, total in enumerate(bases):
            for n in range(n_ch):
                total = total + cprep_v[3 + n] * gathered[n * c1:(n + 1) * c1, t * LANES:(t + 1) * LANES]
            totals.append(total)
        return jnp.concatenate(totals, 1)

    def per_half(x, coeff, op):
        return jnp.concatenate([op(part, coeff) for part in halves(x)], 1)

    solution = per_half(OMEGA * rhs, diag, lambda x, c: x / c)
    for cycle_index in range(CYCLES):
        for sweep_index in range(PRE):
            if cycle_index == 0 and sweep_index == 0:
                continue
            step = OMEGA * (rhs - fine_apply(solution))
            solution = solution + per_half(step, diag, lambda x, c: x / c)
        residual = rhs - fine_apply(solution)
        weighted = per_half(residual, w, lambda x, c: x * c)
        coarse_source = mm(at, weighted)
        correction = per_half(OMEGA * coarse_source, cdiag, lambda x, c: x / c)
        for coarse_sweep_index in range(CSWEEPS - 1):
            step = OMEGA * (coarse_source - coarse_apply(correction))
            correction = correction + per_half(step, cdiag, lambda x, c: x / c)
        lifted = mm(a, correction)
        solution = solution + per_half(lifted, w, lambda x, c: x * c)
        for sweep_index in range(POST):
            step = OMEGA * (rhs - fine_apply(solution))
            solution = solution + per_half(step, diag, lambda x, c: x / c)
    for t, part in enumerate(halves(solution)):
        out_v[0, t] = jnp.transpose(part)[:layers]
    store = pltpu.make_async_copy(out_v, out_hbm, load_sem.at[len(loads)])
    store.start()
    store.wait()


def body(
    right_side,
    absorption,
    vertical,
    horizontal,
    neighbours,
    send_index,
    aggregate,
    weights,
    coarse_vertical,
    coarse_horizontal,
    coarse_neighbours,
    *,
    n_parts,
    n_grp,
):
    _, tracers, layers, columns = right_side.shape
    reach = send_index.shape[1] // 2
    width = send_index.shape[2]
    c1 = coarse_neighbours.shape[2]
    n_slots = 2 * reach

    cvert = coarse_vertical[0]
    chor = coarse_horizontal[0]
    coarse_diagonal = (
        0.5 + jnp.abs(cvert[0]) + jnp.abs(cvert[1]) + jnp.sum(jnp.abs(chor), axis=0)
    )
    layer = lax.broadcasted_iota(jnp.int32, (layers, 1), 0)
    cv0 = jnp.where(layer == 0, 0.0, cvert[0])
    cv1 = jnp.where(layer == layers - 1, 0.0, cvert[1])
    stacked = jnp.concatenate([coarse_diagonal[None], cv0[None], cv1[None], chor], 0)
    fill = jnp.concatenate(
        [
            jnp.ones((1, c1, LANES - layers), F32),
            jnp.zeros((2 + chor.shape[0], c1, LANES - layers), F32),
        ],
        0,
    )
    cprep = jnp.concatenate([jnp.transpose(stacked, (0, 2, 1)), fill], 2)

    si = send_index.reshape(1, n_slots * width)
    n_crow = coarse_neighbours.shape[1] * c1
    cnb = jnp.pad(
        coarse_neighbours.reshape(1, n_crow), ((0, 0), (0, LANES - n_crow)), constant_values=-1
    )

    args = (right_side, absorption, vertical, horizontal, weights, neighbours[0], si, aggregate, cnb, cprep)
    ext_rows = columns + n_slots * width
    coarse_rows = ext_rows
    scratch = [pltpu.VMEM(x.shape, x.dtype) for x in args] + [
        pltpu.VMEM(right_side.shape, F32),
        pltpu.SemaphoreType.DMA((len(args) + 1,)),
        pltpu.VMEM((neighbours.shape[1] * columns, ext_rows), F32),
        pltpu.VMEM((2, n_slots * width, tracers * LANES), F32),
        pltpu.VMEM((n_slots * width, tracers * LANES), F32),
        pltpu.VMEM((2, coarse_rows, tracers * LANES), F32),
        pltpu.SemaphoreType.DMA((n_slots,)),
        pltpu.SemaphoreType.DMA((2, n_slots)),
        pltpu.SemaphoreType.DMA((n_slots,)),
        pltpu.SemaphoreType.DMA((2, n_slots)),
    ]
    return pl.pallas_call(
        functools.partial(vcycle_kernel, n_parts, n_grp, reach, width),
        out_shape=jax.ShapeDtypeStruct(right_side.shape, F32),
        in_specs=[pl.BlockSpec(memory_space=pl.ANY)] * len(args),
        out_specs=pl.BlockSpec(memory_space=pl.ANY),
        scratch_shapes=scratch,
        compiler_params=pltpu.CompilerParams(collective_id=0, has_side_effects=True),
    )(*args)


def solution(mesh):
    placed = (
        P(("dom", "grp"), None, None, None),
        P(("dom", "grp"), None, None),
        P(("dom", "grp"), None, None, None),
        P(("dom", "grp"), None, None, None),
        P(("dom", "grp"), None, None),
        P(("dom", "grp"), None, None),
        P(("dom", "grp"), None),
        P(("dom", "grp"), None, None),
        P(("dom", "grp"), None, None, None),
        P(("dom", "grp"), None, None, None),
        P(("dom", "grp"), None, None),
    )
    n_grp = mesh.shape["grp"]
    n_parts = mesh.shape["dom"] * n_grp
    return jax.shard_map(
        functools.partial(body, n_parts=n_parts, n_grp=n_grp),
        mesh=mesh,
        in_specs=placed,
        out_specs=P(("dom", "grp"), None, None, None),
        check_vma=False,
    )
```

time: 129 us -> 128 us (level)
  Pallas kernels: 110 us -> 120 us
  local copies, waits for them, and re-layouts: 12 us -> 5.7 us
  other arithmetic: 5.65 us -> 1.64 us
    pallas_call x1, Pallas kernels: 110 us -> 120 us  [body(): pl.pallas_call(functools.partial(vcycle_kernel, n_parts, n_grp, reach, wi...]
    convert_element_type x5 -> x0, other arithmetic: 3.79 us -> none  [the longest x2 1.31 us: body(): (aggregate[0][None, :] == jnp.arange(c1, dtype=jnp.int32)[:, None]).astyp...]
    pad x8 -> x1, local copies, waits for them, and re-layouts: 4.33 us -> 0.59 us  [body(): jnp.pad(coarse_neighbours.reshape(1, n_crow), ((0, 0), (0, LANES - n_crow...]
    unnamed x44 -> x12, local copies, waits for them, and re-layouts: 4.35 us -> 3.76 us
where the time goes in v2:
time: 128 us; the launch traced here: 127 us
  Pallas kernels  120 us (94%)
  local copies, waits for them, and re-layouts  5.7 us (4%)
  other arithmetic  1.64 us (1%)
    pallas_call x1, Pallas kernels, body(): pl.pallas_call(functools.partial(vcycle_kernel, n_parts, n_grp, reach, wi...  120 us
    unnamed x12, local copies, waits for them, and re-layouts  3.76 us

profile of v2, /device:TPU:32, one launch (start us, length us, event | category | flops | bytes accessed | tf_op | source)
XLA Modules:
  0.0 127.2 jit_solution(12013002899468598007)
XLA Ops:
  0.0 1.3 reshape.111.si_hbm
  1.3 0.0 copy-start.3
  1.3 0.7 copy-done.3
  2.0 0.0 copy-start.4
  2.0 0.6 copy.14
  2.6 0.1 copy-done.4
  2.7 0.1 reshape.112
  2.7 0.0 copy-start.2
  2.7 0.6 pad.4.cnb_hbm
  3.3 0.0 copy-start
  3.3 0.9 abs_reduce_fusion
  4.2 0.0 copy-done.2
  4.2 0.0 copy-done
  4.3 0.0 copy-start.1
  4.3 0.9 copy-done.1
  5.1 0.7 pad_maximum_fusion.cprep_hbm
  5.9 119.8 %shard_map.109 = f32[1,2,80,128]{3,2,1,0:T(8,128)} custom-call(f32[1,2,80,128]{3,2,1,0:T(8,128)} %rhs_hbm.1, f32[1,80,128]{2,1,0:T(8,128)} %absorption_hbm.1, f32[1,2,80,128]{3,2,1,0:T(8,128)} %vertical_hbm.1, f32[1,6,80,128]{3,2,1,0:T(8,128)} %horizontal_hbm.1, f32[1,80,128]{2,1,0:T(8,128)} %weights_hbm.1, s32[6,128]{1,0:T(8,128)} %bitcast.24, ...), custom_call_target="tpu_custom_call" | custom-call | tf_op jit(solution)/shard_map/pallas_call | solution.py:341
  125.7 1.5 %copy.16 = f32[1,2,80,128]{3,2,1,0:T(8,128)} copy(f32[1,2,80,128]{3,2,1,0:T(8,128)} %shard_map.109) | data formatting | bytes 163840
  (4 shorter events, 0.0 us)
Async XLA Ops:
  1.3 0.7 copy-start.3
  2.0 0.7 copy-start.4
  2.7 1.5 %copy-start.2 = (f32[1,2,80,16]{2,3,1,0:T(8,128)S(1)}, f32[1,2,80,16]{2,3,1,0:T(8,128)}, u32[]{:S(2)}) copy-start(f32[1,2,80,16]{2,3,1,0:T(8,128)} %param.19) | copy-start | bytes 30724
  3.3 0.9 copy-start
  4.3 0.9 copy-start.1

commit v3 on v2

--- a/solution.py
+++ b/solution.py
@@ -17,10 +17,20 @@
 MESH = pl.DeviceIdType.MESH
 LANES = 128
 F32 = jnp.float32
+BF16 = jnp.bfloat16
 
 
 def mm(a, b):
     return jnp.dot(a, b, precision=HIGHEST, preferred_element_type=F32)
+
+
+def select(onehot, x):
+    hi = x.astype(BF16)
+    rest = x - hi.astype(F32)
+    mid = rest.astype(BF16)
+    lo = (rest - mid.astype(F32)).astype(BF16)
+    part = lambda y: jnp.dot(onehot, y, preferred_element_type=F32)
+    return (part(hi) + part(mid)) + part(lo)
 
 
 def vcycle_kernel(
@@ -147,8 +157,8 @@
     k_iota = lax.broadcasted_iota(jnp.int32, (ext_rows, columns), 0)
     for n in range(n_nb):
         chosen = (k_iota == nb_v[n:n + 1, :]).astype(F32)
-        mt_s[pl.ds(n * columns, columns), :] = jnp.transpose(chosen)
-    st = jnp.transpose((lax.broadcasted_iota(jnp.int32, (columns, halo), 0) == si_v[...]).astype(F32))
+        mt_s[pl.ds(n * columns, columns), :] = jnp.transpose(chosen).astype(BF16)
+    st = jnp.transpose((lax.broadcasted_iota(jnp.int32, (columns, halo), 0) == si_v[...]).astype(F32)).astype(BF16)
     at = (lax.broadcasted_iota(jnp.int32, (c1, columns), 0) == agg_v[...]).astype(F32)
     a_full = jnp.transpose((lax.broadcasted_iota(jnp.int32, (LANES, columns), 0) == agg_v[...]).astype(F32))
     a = a_full[:, :c1]
@@ -156,7 +166,7 @@
     n_crow = n_ch * c1
     mct = jnp.transpose(
         (lax.broadcasted_iota(jnp.int32, (coarse_rows, cnb_v.shape[1]), 0) == cnb_v[...]).astype(F32)
-    )[:n_crow]
+    )[:n_crow].astype(BF16)
 
     cdiag = cprep_v[0]
     cv0 = cprep_v[1]
@@ -181,12 +191,12 @@
     def fine_apply(field):
         slot = fine_round[0] % 2
         fine_round[0] += 1
-        sendbuf[...] = mm(st, field)
+        sendbuf[...] = select(st, field)
         for s in range(n_slots):
             @pl.when(valid(me + offsets[s]))
             def _():
                 fine_copy(slot, s).start()
-        local = mm(mt_s[:, pl.ds(0, columns)], field)
+        local = select(mt_s[:, pl.ds(0, columns)], field)
         bases = []
         for part in halves(field):
             lower, upper = shifted(part)
@@ -199,7 +209,7 @@
             @pl.when(valid(me - offsets[s]))
             def _():
                 fine_copy(slot, s).wait_recv()
-        gathered = local + mm(mt_s[:, pl.ds(columns, halo)], ghost[slot])
+        gathered = local + select(mt_s[:, pl.ds(columns, halo)], ghost[slot])
         totals = []
         for t, total in enumerate(bases):
             for n in range(n_nb):
@@ -240,7 +250,7 @@
             @pl.when(valid(me - offsets[k]))
             def _():
                 coarse_copy(slot, k).wait_recv()
-        gathered = mm(mct, cext[slot])
+        gathered = select(mct, cext[slot])
         totals = []
         for t, total in enumerate(bases):
             for n in range(n_ch):
@@ -329,7 +339,7 @@
     scratch = [pltpu.VMEM(x.shape, x.dtype) for x in args] + [
         pltpu.VMEM(right_side.shape, F32),
         pltpu.SemaphoreType.DMA((len(args) + 1,)),
-        pltpu.VMEM((neighbours.shape[1] * columns, ext_rows), F32),
+        pltpu.VMEM((neighbours.shape[1] * columns, ext_rows), BF16),
         pltpu.VMEM((2, n_slots * width, tracers * LANES), F32),
         pltpu.VMEM((n_slots * width, tracers * LANES), F32),
         pltpu.VMEM((2, coarse_rows, tracers * LANES), F32),

time: 128 us -> 110 us (0.86)
  Pallas kernels: 120 us -> 103 us
    pallas_call x1, Pallas kernels: 120 us -> 103 us  [body(): pl.pallas_call(functools.partial(vcycle_kernel, n_parts, n_grp, reach, wi...]
where the time goes in v3:
time: 110 us
  Pallas kernels  103 us (94%)
  local copies, waits for them, and re-layouts  5.7 us (5%)
  other arithmetic  1.64 us (1%)
    pallas_call x1, Pallas kernels, body(): pl.pallas_call(functools.partial(vcycle_kernel, n_parts, n_grp, reach, wi...  103 us
    unnamed x12, local copies, waits for them, and re-layouts  3.76 us

profile of v3, /device:TPU:32, one launch (start us, length us, event | category | flops | bytes accessed | tf_op | source)
XLA Modules:
  0.0 110.0 jit_solution(2284354210567044951)
XLA Ops:
  0.0 1.3 %reshape.111.si_hbm = s32[1,128]{1,0:T(1,128)} reshape(s32[1,8,16]{2,1,0:T(8,128)} %param.16) | data formatting | bytes 1024 | tf_op jit(solution)/shard_map/reshape | solution.py:330
  1.3 0.0 copy-start.3
  1.3 0.7 copy-done.3
  2.0 0.0 copy-start.4
  2.0 0.6 copy.14
  2.6 0.1 copy-done.4
  2.7 0.1 reshape.112
  2.7 0.0 copy-start.2
  2.7 0.6 pad.4.cnb_hbm
  3.3 0.0 copy-start
  3.3 0.9 abs_reduce_fusion
  4.2 0.0 copy-done.2
  4.2 0.0 copy-done
  4.3 0.0 copy-start.1
  4.3 0.9 copy-done.1
  5.1 0.7 pad_maximum_fusion.cprep_hbm
  5.9 102.6 %shard_map.109 = f32[1,2,80,128]{3,2,1,0:T(8,128)} custom-call(f32[1,2,80,128]{3,2,1,0:T(8,128)} %rhs_hbm.1, f32[1,80,128]{2,1,0:T(8,128)} %absorption_hbm.1, f32[1,2,80,128]{3,2,1,0:T(8,128)} %vertical_hbm.1, f32[1,6,80,128]{3,2,1,0:T(8,128)} %horizontal_hbm.1, f32[1,80,128]{2,1,0:T(8,128)} %weights_hbm.1, s32[6,128]{1,0:T(8,128)} %bitcast.24, ...), custom_call_target="tpu_custom_call" | custom-call | tf_op jit(solution)/shard_map/pallas_call | solution.py:351
  108.5 1.5 %copy.16 = f32[1,2,80,128]{3,2,1,0:T(8,128)} copy(f32[1,2,80,128]{3,2,1,0:T(8,128)} %shard_map.109) | data formatting | bytes 163840
  (4 shorter events, 0.0 us)
Async XLA Ops:
  1.3 0.7 copy-start.3
  2.0 0.7 copy-start.4
  2.7 1.5 %copy-start.2 = (f32[1,2,80,16]{2,3,1,0:T(8,128)S(1)}, f32[1,2,80,16]{2,3,1,0:T(8,128)}, u32[]{:S(2)}) copy-start(f32[1,2,80,16]{2,3,1,0:T(8,128)} %param.19) | copy-start | bytes 30724
  3.3 0.9 copy-start
  4.3 0.9 copy-start.1

commit v4 on v3

--- a/solution.py
+++ b/solution.py
@@ -113,9 +113,6 @@
         @pl.when(valid(me + d))
         def _():
             pl.semaphore_signal(barrier, 1, device_id=device(me + d), device_id_type=MESH)
-    peers = sum(valid(me + d).astype(jnp.int32) for d in offsets)
-    pl.semaphore_wait(barrier, peers)
-
     for copy in loads:
         copy.wait()
 
@@ -187,10 +184,22 @@
         )
 
     fine_round = [0]
+    pending = {"fine": None, "coarse": None}
+
+    def finish_sends(kind, copy_of):
+        slot = pending[kind]
+        if slot is None:
+            return
+        pending[kind] = None
+        for s in range(n_slots):
+            @pl.when(valid(me + offsets[s]))
+            def _():
+                copy_of(slot, s).wait_send()
 
     def fine_apply(field):
         slot = fine_round[0] % 2
         fine_round[0] += 1
+        finish_sends("fine", fine_copy)
         sendbuf[...] = select(st, field)
         for s in range(n_slots):
             @pl.when(valid(me + offsets[s]))
@@ -201,11 +210,8 @@
         for part in halves(field):
             lower, upper = shifted(part)
             bases.append(diag * part + v0 * lower + v1 * upper)
+        pending["fine"] = slot
         for s in range(n_slots):
-            @pl.when(valid(me + offsets[s]))
-            def _():
-                fine_copy(slot, s).wait_send()
-
             @pl.when(valid(me - offsets[s]))
             def _():
                 fine_copy(slot, s).wait_recv()
@@ -233,6 +239,7 @@
     def coarse_apply(corr):
         slot = coarse_round[0] % 2
         coarse_round[0] += 1
+        finish_sends("coarse", coarse_copy)
         cext[slot, pl.ds(reach * c1, c1), :] = corr
         for k in range(n_slots):
             @pl.when(valid(me + offsets[k]))
@@ -242,11 +249,8 @@
         for part in halves(corr):
             lower, upper = shifted(part)
             bases.append(cdiag * part + cv0 * lower + cv1 * upper)
+        pending["coarse"] = slot
         for k in range(n_slots):
-            @pl.when(valid(me + offsets[k]))
-            def _():
-                coarse_copy(slot, k).wait_send()
-
             @pl.when(valid(me - offsets[k]))
             def _():
                 coarse_copy(slot, k).wait_recv()
@@ -257,6 +261,9 @@
                 total = total + cprep_v[3 + n] * gathered[n * c1:(n + 1) * c1, t * LANES:(t + 1) * LANES]
             totals.append(total)
         return jnp.concatenate(totals, 1)
+
+    peers = sum(valid(me + d).astype(jnp.int32) for d in offsets)
+    pl.semaphore_wait(barrier, peers)
 
     def per_half(x, coeff, op):
         return jnp.concatenate([op(part, coeff) for part in halves(x)], 1)
@@ -280,6 +287,8 @@
         for sweep_index in range(POST):
             step = OMEGA * (rhs - fine_apply(solution))
             solution = solution + per_half(step, diag, lambda x, c: x / c)
+    finish_sends("fine", fine_copy)
+    finish_sends("coarse", coarse_copy)
     for t, part in enumerate(halves(solution)):
         out_v[0, t] = jnp.transpose(part)[:layers]
     store = pltpu.make_async_copy(out_v, out_hbm, load_sem.at[len(loads)])

time: 110 us -> 110 us (level)
  no operation moved by 1% of the time
where the time goes in v4:
time: 110 us
  Pallas kernels  102 us (93%)
  local copies, waits for them, and re-layouts  5.7 us (5%)
  other arithmetic  1.64 us (1%)
    pallas_call x1, Pallas kernels, body(): pl.pallas_call(functools.partial(vcycle_kernel, n_parts, n_grp, reach, wi...  102 us
    unnamed x12, local copies, waits for them, and re-layouts  3.76 us

profile of v4, /device:TPU:32, one launch (start us, length us, event | category | flops | bytes accessed | tf_op | source)
XLA Modules:
  0.0 109.8 jit_solution(13682773334871134618)
XLA Ops:
  0.0 1.3 %reshape.111.si_hbm = s32[1,128]{1,0:T(1,128)} reshape(s32[1,8,16]{2,1,0:T(8,128)} %param.16) | data formatting | bytes 1024 | tf_op jit(solution)/shard_map/reshape | solution.py:339
  1.3 0.0 copy-start.3
  1.3 0.7 copy-done.3
  2.0 0.0 copy-start.4
  2.0 0.6 copy.14
  2.6 0.1 copy-done.4
  2.7 0.1 reshape.112
  2.7 0.0 copy-start.2
  2.7 0.6 pad.4.cnb_hbm
  3.3 0.0 copy-start
  3.3 0.9 abs_reduce_fusion
  4.2 0.0 copy-done.2
  4.2 0.0 copy-done
  4.3 0.0 copy-start.1
  4.3 0.9 copy-done.1
  5.1 0.7 pad_maximum_fusion.cprep_hbm
  5.9 102.4 %shard_map.109 = f32[1,2,80,128]{3,2,1,0:T(8,128)} custom-call(f32[1,2,80,128]{3,2,1,0:T(8,128)} %rhs_hbm.1, f32[1,80,128]{2,1,0:T(8,128)} %absorption_hbm.1, f32[1,2,80,128]{3,2,1,0:T(8,128)} %vertical_hbm.1, f32[1,6,80,128]{3,2,1,0:T(8,128)} %horizontal_hbm.1, f32[1,80,128]{2,1,0:T(8,128)} %weights_hbm.1, s32[6,128]{1,0:T(8,128)} %bitcast.24, ...), custom_call_target="tpu_custom_call" | custom-call | tf_op jit(solution)/shard_map/pallas_call | solution.py:360
  108.3 1.5 %copy.16 = f32[1,2,80,128]{3,2,1,0:T(8,128)} copy(f32[1,2,80,128]{3,2,1,0:T(8,128)} %shard_map.109) | data formatting | bytes 163840
  (4 shorter events, 0.0 us)
Async XLA Ops:
  1.3 0.7 copy-start.3
  2.0 0.7 copy-start.4
  2.7 1.5 %copy-start.2 = (f32[1,2,80,16]{2,3,1,0:T(8,128)S(1)}, f32[1,2,80,16]{2,3,1,0:T(8,128)}, u32[]{:S(2)}) copy-start(f32[1,2,80,16]{2,3,1,0:T(8,128)} %param.19) | copy-start | bytes 30724
  3.3 0.9 copy-start
  4.3 0.9 copy-start.1

commit v5 on v4

--- a/solution.py
+++ b/solution.py
@@ -26,11 +26,9 @@
 
 def select(onehot, x):
     hi = x.astype(BF16)
-    rest = x - hi.astype(F32)
-    mid = rest.astype(BF16)
-    lo = (rest - mid.astype(F32)).astype(BF16)
+    lo = (x - hi.astype(F32)).astype(BF16)
     part = lambda y: jnp.dot(onehot, y, preferred_element_type=F32)
-    return (part(hi) + part(mid)) + part(lo)
+    return part(hi) + part(lo)
 
 
 def vcycle_kernel(
@@ -165,7 +163,9 @@
         (lax.broadcasted_iota(jnp.int32, (coarse_rows, cnb_v.shape[1]), 0) == cnb_v[...]).astype(F32)
     )[:n_crow].astype(BF16)
 
+    inv_diag = 1.0 / diag
     cdiag = cprep_v[0]
+    inv_cdiag = 1.0 / cdiag
     cv0 = cprep_v[1]
     cv1 = cprep_v[2]
 
@@ -207,15 +207,18 @@
                 fine_copy(slot, s).start()
         local = select(mt_s[:, pl.ds(0, columns)], field)
         bases = []
-        for part in halves(field):
+        for t, part in enumerate(halves(field)):
             lower, upper = shifted(part)
-            bases.append(diag * part + v0 * lower + v1 * upper)
+            total = diag * part + v0 * lower + v1 * upper
+            for n in range(n_nb):
+                total = total + h[n] * local[n * columns:(n + 1) * columns, t * LANES:(t + 1) * LANES]
+            bases.append(total)
         pending["fine"] = slot
         for s in range(n_slots):
             @pl.when(valid(me - offsets[s]))
             def _():
                 fine_copy(slot, s).wait_recv()
-        gathered = local + select(mt_s[:, pl.ds(columns, halo)], ghost[slot])
+        gathered = select(mt_s[:, pl.ds(columns, halo)], ghost[slot])
         totals = []
         for t, total in enumerate(bases):
             for n in range(n_nb):
@@ -268,25 +271,25 @@
     def per_half(x, coeff, op):
         return jnp.concatenate([op(part, coeff) for part in halves(x)], 1)
 
-    solution = per_half(OMEGA * rhs, diag, lambda x, c: x / c)
+    solution = per_half(OMEGA * rhs, inv_diag, lambda x, c: x * c)
     for cycle_index in range(CYCLES):
         for sweep_index in range(PRE):
             if cycle_index == 0 and sweep_index == 0:
                 continue
             step = OMEGA * (rhs - fine_apply(solution))
-            solution = solution + per_half(step, diag, lambda x, c: x / c)
+            solution = solution + per_half(step, inv_diag, lambda x, c: x * c)
         residual = rhs - fine_apply(solution)
         weighted = per_half(residual, w, lambda x, c: x * c)
         coarse_source = mm(at, weighted)
-        correction = per_half(OMEGA * coarse_source, cdiag, lambda x, c: x / c)
+        correction = per_half(OMEGA * coarse_source, inv_cdiag, lambda x, c: x * c)
         for coarse_sweep_index in range(CSWEEPS - 1):
             step = OMEGA * (coarse_source - coarse_apply(correction))
-            correction = correction + per_half(step, cdiag, lambda x, c: x / c)
+            correction = correction + per_half(step, inv_cdiag, lambda x, c: x * c)
         lifted = mm(a, correction)
         solution = solution + per_half(lifted, w, lambda x, c: x * c)
         for sweep_index in range(POST):
             step = OMEGA * (rhs - fine_apply(solution))
-            solution = solution + per_half(step, diag, lambda x, c: x / c)
+            solution = solution + per_half(step, inv_diag, lambda x, c: x * c)
     finish_sends("fine", fine_copy)
     finish_sends("coarse", coarse_copy)
     for t, part in enumerate(halves(solution)):

time: 110 us -> 108 us (0.982)
  Pallas kernels: 102 us -> 100 us
    pallas_call x1, Pallas kernels: 102 us -> 100 us  [body(): pl.pallas_call(functools.partial(vcycle_kernel, n_parts, n_grp, reach, wi...]
where the time goes in v5:
time: 108 us
  Pallas kernels  100 us (93%)
  local copies, waits for them, and re-layouts  5.7 us (5%)
  other arithmetic  1.64 us (2%)
    pallas_call x1, Pallas kernels, body(): pl.pallas_call(functools.partial(vcycle_kernel, n_parts, n_grp, reach, wi...  100 us
    unnamed x12, local copies, waits for them, and re-layouts  3.76 us

profile of v5, /device:TPU:32, one launch (start us, length us, event | category | flops | bytes accessed | tf_op | source)
XLA Modules:
  0.0 107.8 jit_solution(14238987311664944778)
XLA Ops:
  0.0 1.3 %reshape.111.si_hbm = s32[1,128]{1,0:T(1,128)} reshape(s32[1,8,16]{2,1,0:T(8,128)} %param.16) | data formatting | bytes 1024 | tf_op jit(solution)/shard_map/reshape | solution.py:342
  1.3 0.0 copy-start.3
  1.3 0.7 copy-done.3
  2.0 0.0 copy-start.4
  2.0 0.6 copy.14
  2.6 0.1 copy-done.4
  2.7 0.1 reshape.112
  2.7 0.0 copy-start.2
  2.7 0.6 pad.4.cnb_hbm
  3.3 0.0 copy-start
  3.3 0.9 abs_reduce_fusion
  4.2 0.0 copy-done.2
  4.2 0.0 copy-done
  4.3 0.0 copy-start.1
  4.3 0.9 copy-done.1
  5.1 0.7 pad_maximum_fusion.cprep_hbm
  5.9 100.4 %shard_map.109 = f32[1,2,80,128]{3,2,1,0:T(8,128)} custom-call(f32[1,2,80,128]{3,2,1,0:T(8,128)} %rhs_hbm.1, f32[1,80,128]{2,1,0:T(8,128)} %absorption_hbm.1, f32[1,2,80,128]{3,2,1,0:T(8,128)} %vertical_hbm.1, f32[1,6,80,128]{3,2,1,0:T(8,128)} %horizontal_hbm.1, f32[1,80,128]{2,1,0:T(8,128)} %weights_hbm.1, s32[6,128]{1,0:T(8,128)} %bitcast.24, ...), custom_call_target="tpu_custom_call" | custom-call | tf_op jit(solution)/shard_map/pallas_call | solution.py:363
  106.2 1.5 %copy.16 = f32[1,2,80,128]{3,2,1,0:T(8,128)} copy(f32[1,2,80,128]{3,2,1,0:T(8,128)} %shard_map.109) | data formatting | bytes 163840
  (4 shorter events, 0.0 us)
Async XLA Ops:
  1.3 0.7 copy-start.3
  2.0 0.7 copy-start.4
  2.7 1.5 %copy-start.2 = (f32[1,2,80,16]{2,3,1,0:T(8,128)S(1)}, f32[1,2,80,16]{2,3,1,0:T(8,128)}, u32[]{:S(2)}) copy-start(f32[1,2,80,16]{2,3,1,0:T(8,128)} %param.19) | copy-start | bytes 30724
  3.3 0.9 copy-start
  4.3 0.9 copy-start.1

commit v6 on v5

--- a/solution.py
+++ b/solution.py
@@ -71,6 +71,7 @@
     me = lax.axis_index("dom") * n_grp + lax.axis_index("grp")
     offsets = list(range(1, reach + 1)) + [-d for d in range(1, reach + 1)]
     n_slots = len(offsets)
+    by_distance = sorted(range(n_slots), key=lambda s: (abs(offsets[s]) != 2, abs(offsets[s]) == reach, abs(offsets[s]), offsets[s] < 0))
     tracers, layers, columns = rhs_v.shape[1:]
     n_nb = nb_v.shape[0]
     c1 = cprep_v.shape[1]
@@ -201,7 +202,7 @@
         fine_round[0] += 1
         finish_sends("fine", fine_copy)
         sendbuf[...] = select(st, field)
-        for s in range(n_slots):
+        for s in by_distance:
             @pl.when(valid(me + offsets[s]))
             def _():
                 fine_copy(slot, s).start()
@@ -244,7 +245,7 @@
         coarse_round[0] += 1
         finish_sends("coarse", coarse_copy)
         cext[slot, pl.ds(reach * c1, c1), :] = corr
-        for k in range(n_slots):
+        for k in by_distance:
             @pl.when(valid(me + offsets[k]))
             def _():
                 coarse_copy(slot, k).start()

time: 108 us -> 108 us (level)
  no operation moved by 1% of the time
where the time goes in v6:
time: 108 us
  Pallas kernels  100 us (93%)
  local copies, waits for them, and re-layouts  5.7 us (5%)
  other arithmetic  1.64 us (2%)
    pallas_call x1, Pallas kernels, body(): pl.pallas_call(functools.partial(vcycle_kernel, n_parts, n_grp, reach, wi...  100 us
    unnamed x12, local copies, waits for them, and re-layouts  3.76 us

profile of v6, /device:TPU:32, one launch (start us, length us, event | category | flops | bytes accessed | tf_op | source)
XLA Modules:
  0.0 107.6 jit_solution(1974938725144908414)
XLA Ops:
  0.0 1.3 %reshape.111.si_hbm = s32[1,128]{1,0:T(1,128)} reshape(s32[1,8,16]{2,1,0:T(8,128)} %param.16) | data formatting | bytes 1024 | tf_op jit(solution)/shard_map/reshape | solution.py:343
  1.3 0.0 copy-start.3
  1.3 0.7 copy-done.3
  2.0 0.0 copy-start.4
  2.0 0.6 copy.14
  2.6 0.1 copy-done.4
  2.7 0.1 reshape.112
  2.7 0.0 copy-start.2
  2.7 0.6 pad.4.cnb_hbm
  3.3 0.0 copy-start
  3.3 0.9 abs_reduce_fusion
  4.2 0.0 copy-done.2
  4.2 0.0 copy-done
  4.3 0.0 copy-start.1
  4.3 0.9 copy-done.1
  5.1 0.7 pad_maximum_fusion.cprep_hbm
  5.9 100.2 %shard_map.109 = f32[1,2,80,128]{3,2,1,0:T(8,128)} custom-call(f32[1,2,80,128]{3,2,1,0:T(8,128)} %rhs_hbm.1, f32[1,80,128]{2,1,0:T(8,128)} %absorption_hbm.1, f32[1,2,80,128]{3,2,1,0:T(8,128)} %vertical_hbm.1, f32[1,6,80,128]{3,2,1,0:T(8,128)} %horizontal_hbm.1, f32[1,80,128]{2,1,0:T(8,128)} %weights_hbm.1, s32[6,128]{1,0:T(8,128)} %bitcast.24, ...), custom_call_target="tpu_custom_call" | custom-call | tf_op jit(solution)/shard_map/pallas_call | solution.py:364
  106.1 1.5 %copy.16 = f32[1,2,80,128]{3,2,1,0:T(8,128)} copy(f32[1,2,80,128]{3,2,1,0:T(8,128)} %shard_map.109) | data formatting | bytes 163840
  (4 shorter events, 0.0 us)
Async XLA Ops:
  1.3 0.7 copy-start.3
  2.0 0.7 copy-start.4
  2.7 1.5 %copy-start.2 = (f32[1,2,80,16]{2,3,1,0:T(8,128)S(1)}, f32[1,2,80,16]{2,3,1,0:T(8,128)}, u32[]{:S(2)}) copy-start(f32[1,2,80,16]{2,3,1,0:T(8,128)} %param.19) | copy-start | bytes 30724
  3.3 0.9 copy-start
  4.3 0.9 copy-start.1

commit v7 on v6

--- a/solution.py
+++ b/solution.py
@@ -24,11 +24,14 @@
     return jnp.dot(a, b, precision=HIGHEST, preferred_element_type=F32)
 
 
-def select(onehot, x):
+def select(onehot2, x):
     hi = x.astype(BF16)
     lo = (x - hi.astype(F32)).astype(BF16)
-    part = lambda y: jnp.dot(onehot, y, preferred_element_type=F32)
-    return part(hi) + part(lo)
+    return jnp.dot(onehot2, jnp.concatenate([hi, lo], 0), preferred_element_type=F32)
+
+
+def doubled(onehot):
+    return jnp.concatenate([onehot, onehot], 1)
 
 
 def vcycle_kernel(
@@ -59,7 +62,8 @@
     cprep_v,
     out_v,
     load_sem,
-    mt_s,
+    mt_local,
+    mt_ghost,
     ghost,
     sendbuf,
     cext,
@@ -152,9 +156,11 @@
     ext_rows = columns + halo
     k_iota = lax.broadcasted_iota(jnp.int32, (ext_rows, columns), 0)
     for n in range(n_nb):
-        chosen = (k_iota == nb_v[n:n + 1, :]).astype(F32)
-        mt_s[pl.ds(n * columns, columns), :] = jnp.transpose(chosen).astype(BF16)
-    st = jnp.transpose((lax.broadcasted_iota(jnp.int32, (columns, halo), 0) == si_v[...]).astype(F32)).astype(BF16)
+        chosen = jnp.transpose((k_iota == nb_v[n:n + 1, :]).astype(F32)).astype(BF16)
+        rows = pl.ds(n * columns, columns)
+        mt_local[rows, :] = doubled(chosen[:, :columns])
+        mt_ghost[rows, :] = doubled(chosen[:, columns:])
+    st = doubled(jnp.transpose((lax.broadcasted_iota(jnp.int32, (columns, halo), 0) == si_v[...]).astype(F32)).astype(BF16))
     at = (lax.broadcasted_iota(jnp.int32, (c1, columns), 0) == agg_v[...]).astype(F32)
     a_full = jnp.transpose((lax.broadcasted_iota(jnp.int32, (LANES, columns), 0) == agg_v[...]).astype(F32))
     a = a_full[:, :c1]
@@ -163,6 +169,7 @@
     mct = jnp.transpose(
         (lax.broadcasted_iota(jnp.int32, (coarse_rows, cnb_v.shape[1]), 0) == cnb_v[...]).astype(F32)
     )[:n_crow].astype(BF16)
+    mct = doubled(mct)
 
     inv_diag = 1.0 / diag
     cdiag = cprep_v[0]
@@ -206,7 +213,7 @@
             @pl.when(valid(me + offsets[s]))
             def _():
                 fine_copy(slot, s).start()
-        local = select(mt_s[:, pl.ds(0, columns)], field)
+        local = select(mt_local[...], field)
         bases = []
         for t, part in enumerate(halves(field)):
             lower, upper = shifted(part)
@@ -219,7 +226,7 @@
             @pl.when(valid(me - offsets[s]))
             def _():
                 fine_copy(slot, s).wait_recv()
-        gathered = select(mt_s[:, pl.ds(columns, halo)], ghost[slot])
+        gathered = select(mt_ghost[...], ghost[slot])
         totals = []
         for t, total in enumerate(bases):
             for n in range(n_nb):
@@ -352,7 +359,8 @@
     scratch = [pltpu.VMEM(x.shape, x.dtype) for x in args] + [
         pltpu.VMEM(right_side.shape, F32),
         pltpu.SemaphoreType.DMA((len(args) + 1,)),
-        pltpu.VMEM((neighbours.shape[1] * columns, ext_rows), BF16),
+        pltpu.VMEM((neighbours.shape[1] * columns, 2 * columns), BF16),
+        pltpu.VMEM((neighbours.shape[1] * columns, 2 * n_slots * width), BF16),
         pltpu.VMEM((2, n_slots * width, tracers * LANES), F32),
         pltpu.VMEM((n_slots * width, tracers * LANES), F32),
         pltpu.VMEM((2, coarse_rows, tracers * LANES), F32),

time: 108 us -> 106 us (0.981)
  Pallas kernels: 100 us -> 98.6 us
    pallas_call x1, Pallas kernels: 100 us -> 98.6 us  [body(): pl.pallas_call(functools.partial(vcycle_kernel, n_parts, n_grp, reach, wi...]
where the time goes in v7:
time: 106 us
  Pallas kernels  98.6 us (93%)
  local copies, waits for them, and re-layouts  5.7 us (5%)
  other arithmetic  1.64 us (2%)
    pallas_call x1, Pallas kernels, body(): pl.pallas_call(functools.partial(vcycle_kernel, n_parts, n_grp, reach, wi...  98.6 us
    unnamed x12, local copies, waits for them, and re-layouts  3.76 us

profile of v7, /device:TPU:32, one launch (start us, length us, event | category | flops | bytes accessed | tf_op | source)
XLA Modules:
  0.0 106.0 jit_solution(7345645015600286303)
XLA Ops:
  0.0 1.3 %reshape.111.si_hbm = s32[1,128]{1,0:T(1,128)} reshape(s32[1,8,16]{2,1,0:T(8,128)} %param.16) | data formatting | bytes 1024 | tf_op jit(solution)/shard_map/reshape | solution.py:350
  1.3 0.0 copy-start.3
  1.3 0.7 copy-done.3
  2.0 0.0 copy-start.4
  2.0 0.6 copy.14
  2.6 0.1 copy-done.4
  2.7 0.1 reshape.112
  2.7 0.0 copy-start.2
  2.7 0.6 pad.4.cnb_hbm
  3.3 0.0 copy-start
  3.3 0.9 abs_reduce_fusion
  4.2 0.0 copy-done.2
  4.2 0.0 copy-done
  4.3 0.0 copy-start.1
  4.3 0.9 copy-done.1
  5.1 0.7 pad_maximum_fusion.cprep_hbm
  5.9 98.6 %shard_map.109 = f32[1,2,80,128]{3,2,1,0:T(8,128)} custom-call(f32[1,2,80,128]{3,2,1,0:T(8,128)} %rhs_hbm.1, f32[1,80,128]{2,1,0:T(8,128)} %absorption_hbm.1, f32[1,2,80,128]{3,2,1,0:T(8,128)} %vertical_hbm.1, f32[1,6,80,128]{3,2,1,0:T(8,128)} %horizontal_hbm.1, f32[1,80,128]{2,1,0:T(8,128)} %weights_hbm.1, s32[6,128]{1,0:T(8,128)} %bitcast.24, ...), custom_call_target="tpu_custom_call" | custom-call | tf_op jit(solution)/shard_map/pallas_call | solution.py:372
  104.4 1.5 %copy.16 = f32[1,2,80,128]{3,2,1,0:T(8,128)} copy(f32[1,2,80,128]{3,2,1,0:T(8,128)} %shard_map.109) | data formatting | bytes 163840
  (4 shorter events, 0.0 us)
Async XLA Ops:
  1.3 0.7 copy-start.3
  2.0 0.7 copy-start.4
  2.7 1.5 %copy-start.2 = (f32[1,2,80,16]{2,3,1,0:T(8,128)S(1)}, f32[1,2,80,16]{2,3,1,0:T(8,128)}, u32[]{:S(2)}) copy-start(f32[1,2,80,16]{2,3,1,0:T(8,128)} %param.19) | copy-start | bytes 30724
  3.3 0.9 copy-start
  4.3 0.9 copy-start.1

commit v8 on v7

--- a/solution.py
+++ b/solution.py
@@ -48,7 +48,8 @@
     si_hbm,
     agg_hbm,
     cnb_hbm,
-    cprep_hbm,
+    cvert_hbm,
+    chor_hbm,
     out_hbm,
     rhs_v,
     absorption_v,
@@ -59,7 +60,8 @@
     si_v,
     agg_v,
     cnb_v,
-    cprep_v,
+    cvert_v,
+    chor_v,
     out_v,
     load_sem,
     mt_local,
@@ -78,8 +80,8 @@
     by_distance = sorted(range(n_slots), key=lambda s: (abs(offsets[s]) != 2, abs(offsets[s]) == reach, abs(offsets[s]), offsets[s] < 0))
     tracers, layers, columns = rhs_v.shape[1:]
     n_nb = nb_v.shape[0]
-    c1 = cprep_v.shape[1]
-    n_ch = cprep_v.shape[0] - 3
+    c1 = cnb_v.shape[2]
+    n_ch = chor_v.shape[1]
     halo = n_slots * width
 
     def valid(q):
@@ -101,7 +103,8 @@
                 (si_hbm, si_v),
                 (agg_hbm, agg_v),
                 (cnb_hbm, cnb_v),
-                (cprep_hbm, cprep_v),
+                (cvert_hbm, cvert_v),
+                (chor_hbm, chor_v),
             ]
         )
     ]
@@ -160,22 +163,39 @@
         rows = pl.ds(n * columns, columns)
         mt_local[rows, :] = doubled(chosen[:, :columns])
         mt_ghost[rows, :] = doubled(chosen[:, columns:])
-    st = doubled(jnp.transpose((lax.broadcasted_iota(jnp.int32, (columns, halo), 0) == si_v[...]).astype(F32)).astype(BF16))
+    st_blocks = []
+    for s in range(n_slots):
+        block = (lax.broadcasted_iota(jnp.int32, (columns, width), 0) == si_v[0, s:s + 1, :]).astype(F32)
+        st_blocks.append(jnp.transpose(block))
+    st = doubled(jnp.concatenate(st_blocks, 0).astype(BF16))
     at = (lax.broadcasted_iota(jnp.int32, (c1, columns), 0) == agg_v[...]).astype(F32)
     a_full = jnp.transpose((lax.broadcasted_iota(jnp.int32, (LANES, columns), 0) == agg_v[...]).astype(F32))
-    a = a_full[:, :c1]
+    a = doubled(a_full[:, :c1].astype(BF16))
     coarse_rows = cext.shape[1]
     n_crow = n_ch * c1
-    mct = jnp.transpose(
-        (lax.broadcasted_iota(jnp.int32, (coarse_rows, cnb_v.shape[1]), 0) == cnb_v[...]).astype(F32)
-    )[:n_crow].astype(BF16)
-    mct = doubled(mct)
-
+    mct_blocks = []
+    for n in range(n_ch):
+        block = (lax.broadcasted_iota(jnp.int32, (coarse_rows, c1), 0) == cnb_v[0, n:n + 1, :]).astype(F32)
+        mct_blocks.append(jnp.transpose(block))
+    mct = doubled(jnp.concatenate(mct_blocks, 0).astype(BF16))
+
+    coarse_pad = jnp.zeros((LANES - layers, c1), F32)
+
+    def coarse_cols(slab):
+        return jnp.transpose(jnp.concatenate([slab, coarse_pad], 0))
+
+    cvr0 = cvert_v[0, 0]
+    cvr1 = cvert_v[0, 1]
+    cdiag_rows = 0.5 + jnp.abs(cvr0) + jnp.abs(cvr1)
+    csum = jnp.abs(chor_v[0, 0])
+    for n in range(1, n_ch):
+        csum = csum + jnp.abs(chor_v[0, n])
+    cdiag = jnp.where(live, coarse_cols(cdiag_rows + csum), 1.0)
+    cv0 = jnp.where(layer_lane == 0, 0.0, coarse_cols(cvr0))
+    cv1 = jnp.where(layer_lane == layers - 1, 0.0, coarse_cols(cvr1))
+    ch = [coarse_cols(chor_v[0, n]) for n in range(n_ch)]
     inv_diag = 1.0 / diag
-    cdiag = cprep_v[0]
     inv_cdiag = 1.0 / cdiag
-    cv0 = cprep_v[1]
-    cv1 = cprep_v[2]
 
     def halves(x):
         return [x[:, t * LANES:(t + 1) * LANES] for t in range(x.shape[1] // LANES)]
@@ -269,7 +289,7 @@
         totals = []
         for t, total in enumerate(bases):
             for n in range(n_ch):
-                total = total + cprep_v[3 + n] * gathered[n * c1:(n + 1) * c1, t * LANES:(t + 1) * LANES]
+                total = total + ch[n] * gathered[n * c1:(n + 1) * c1, t * LANES:(t + 1) * LANES]
             totals.append(total)
         return jnp.concatenate(totals, 1)
 
@@ -293,7 +313,7 @@
         for coarse_sweep_index in range(CSWEEPS - 1):
             step = OMEGA * (coarse_source - coarse_apply(correction))
             correction = correction + per_half(step, inv_cdiag, lambda x, c: x * c)
-        lifted = mm(a, correction)
+        lifted = select(a, correction)
         solution = solution + per_half(lifted, w, lambda x, c: x * c)
         for sweep_index in range(POST):
             step = OMEGA * (rhs - fine_apply(solution))
@@ -329,31 +349,7 @@
     c1 = coarse_neighbours.shape[2]
     n_slots = 2 * reach
 
-    cvert = coarse_vertical[0]
-    chor = coarse_horizontal[0]
-    coarse_diagonal = (
-        0.5 + jnp.abs(cvert[0]) + jnp.abs(cvert[1]) + jnp.sum(jnp.abs(chor), axis=0)
-    )
-    layer = lax.broadcasted_iota(jnp.int32, (layers, 1), 0)
-    cv0 = jnp.where(layer == 0, 0.0, cvert[0])
-    cv1 = jnp.where(layer == layers - 1, 0.0, cvert[1])
-    stacked = jnp.concatenate([coarse_diagonal[None], cv0[None], cv1[None], chor], 0)
-    fill = jnp.concatenate(
-        [
-            jnp.ones((1, c1, LANES - layers), F32),
-            jnp.zeros((2 + chor.shape[0], c1, LANES - layers), F32),
-        ],
-        0,
-    )
-    cprep = jnp.concatenate([jnp.transpose(stacked, (0, 2, 1)), fill], 2)
-
-    si = send_index.reshape(1, n_slots * width)
-    n_crow = coarse_neighbours.shape[1] * c1
-    cnb = jnp.pad(
-        coarse_neighbours.reshape(1, n_crow), ((0, 0), (0, LANES - n_crow)), constant_values=-1
-    )
-
-    args = (right_side, absorption, vertical, horizontal, weights, neighbours[0], si, aggregate, cnb, cprep)
+    args = (right_side, absorption, vertical, horizontal, weights, neighbours[0], send_index, aggregate, coarse_neighbours, coarse_vertical, coarse_horizontal)
     ext_rows = columns + n_slots * width
     coarse_rows = ext_rows
     scratch = [pltpu.VMEM(x.shape, x.dtype) for x in args] + [

time: 106 us -> 104 us (0.981)
  other arithmetic: 1.64 us -> 0 us
    unnamed x12 -> x9, local copies, waits for them, and re-layouts: 3.76 us -> 5.67 us
    reshape x2 -> x0, local copies, waits for them, and re-layouts: 1.35 us -> none  [the longest x1 1.27 us: body(): si = send_index.reshape(1, n_slots * width)]
where the time goes in v8:
time: 104 us
  Pallas kernels  98.1 us (94%)
  local copies, waits for them, and re-layouts  5.67 us (5%)
    pallas_call x1, Pallas kernels, body(): pl.pallas_call(functools.partial(vcycle_kernel, n_parts, n_grp, reach, wi...  98.1 us
    unnamed x9, local copies, waits for them, and re-layouts  5.67 us

profile of v8, /device:TPU:32, one launch (start us, length us, event | category | flops | bytes accessed | tf_op | source)
XLA Modules:
  0.0 103.8 jit_solution(13493900883782846111)
XLA Ops:
  0.0 0.0 copy-start.1
  0.0 1.3 %copy.17 = s32[1,6,128]{2,1,0:T(8,128)} copy(s32[1,6,128]{2,0,1:T(1,128)} %param.15) | data formatting | bytes 6144
  1.3 0.0 copy-done.1
  1.3 0.6 copy.12.cnb_hbm
  1.9 0.0 copy-start
  1.9 1.4 %copy.13.cvert_hbm = f32[1,2,80,16]{3,2,1,0:T(8,128)} copy(f32[1,2,80,16]{2,3,1,0:T(8,128)} %param.19) | data formatting | bytes 20480 | tf_op args[8]
  3.3 0.0 copy-done
  3.3 0.8 copy.14.chor_hbm
  4.2 98.1 %shard_map.109 = f32[1,2,80,128]{3,2,1,0:T(8,128)} custom-call(f32[1,2,80,128]{3,2,1,0:T(8,128)} %rhs_hbm.1, f32[1,80,128]{2,1,0:T(8,128)} %absorption_hbm.1, f32[1,2,80,128]{3,2,1,0:T(8,128)} %vertical_hbm.1, f32[1,6,80,128]{3,2,1,0:T(8,128)} %horizontal_hbm.1, f32[1,80,128]{2,1,0:T(8,128)} %weights_hbm.1, s32[6,128]{1,0:T(8,128)} %bitcast.3, ...), custom_call_target="tpu_custom_call" | custom-call | tf_op jit(solution)/shard_map/pallas_call | solution.py:368
  102.3 1.5 %copy.19 = f32[1,2,80,128]{3,2,1,0:T(8,128)} copy(f32[1,2,80,128]{3,2,1,0:T(8,128)} %shard_map.109) | data formatting | bytes 163840
Async XLA Ops:
  0.0 1.3 %copy-start.1 = (s32[1,6,16]{2,0,1:T(1,128)S(1)}, s32[1,6,16]{2,0,1:T(1,128)}, u32[]{:S(2)}) copy-start(s32[1,6,16]{2,0,1:T(1,128)} %param.21) | copy-start | bytes 1156
  1.9 1.4 %copy-start = (f32[1,6,80,16]{2,3,1,0:T(8,128)S(1)}, f32[1,6,80,16]{2,3,1,0:T(8,128)}, u32[]{:S(2)}) copy-start(f32[1,6,80,16]{2,3,1,0:T(8,128)} %param.20) | copy-start | bytes 92164

commit v9 on v8

--- a/solution.py
+++ b/solution.py
@@ -159,7 +159,7 @@
     ext_rows = columns + halo
     k_iota = lax.broadcasted_iota(jnp.int32, (ext_rows, columns), 0)
     for n in range(n_nb):
-        chosen = jnp.transpose((k_iota == nb_v[n:n + 1, :]).astype(F32)).astype(BF16)
+        chosen = jnp.transpose((k_iota == nb_v[n]).astype(F32)).astype(BF16)
         rows = pl.ds(n * columns, columns)
         mt_local[rows, :] = doubled(chosen[:, :columns])
         mt_ghost[rows, :] = doubled(chosen[:, columns:])
@@ -175,14 +175,16 @@
     n_crow = n_ch * c1
     mct_blocks = []
     for n in range(n_ch):
-        block = (lax.broadcasted_iota(jnp.int32, (coarse_rows, c1), 0) == cnb_v[0, n:n + 1, :]).astype(F32)
+        block = (lax.broadcasted_iota(jnp.int32, (coarse_rows, c1), 0) == cnb_v[n]).astype(F32)
         mct_blocks.append(jnp.transpose(block))
     mct = doubled(jnp.concatenate(mct_blocks, 0).astype(BF16))
 
-    coarse_pad = jnp.zeros((LANES - layers, c1), F32)
+    widen = (
+        lax.broadcasted_iota(jnp.int32, (layers, LANES), 0) == lax.broadcasted_iota(jnp.int32, (layers, LANES), 1)
+    ).astype(F32)
 
     def coarse_cols(slab):
-        return jnp.transpose(jnp.concatenate([slab, coarse_pad], 0))
+        return mm(slab, widen)
 
     cvr0 = cvert_v[0, 0]
     cvr1 = cvert_v[0, 1]
@@ -349,7 +351,19 @@
     c1 = coarse_neighbours.shape[2]
     n_slots = 2 * reach
 
-    args = (right_side, absorption, vertical, horizontal, weights, neighbours[0], send_index, aggregate, coarse_neighbours, coarse_vertical, coarse_horizontal)
+    args = (
+        right_side,
+        absorption,
+        vertical,
+        horizontal,
+        weights,
+        jnp.swapaxes(neighbours, 0, 1),
+        send_index,
+        aggregate,
+        jnp.swapaxes(coarse_neighbours, 0, 1),
+        jnp.swapaxes(coarse_vertical, 2, 3),
+        jnp.swapaxes(coarse_horizontal, 2, 3),
+    )
     ext_rows = columns + n_slots * width
     coarse_rows = ext_rows
     scratch = [pltpu.VMEM(x.shape, x.dtype) for x in args] + [

time: 104 us -> 99.9 us (0.961)
  local copies, waits for them, and re-layouts: 5.67 us -> 1.53 us
    unnamed x9 -> x1, local copies, waits for them, and re-layouts: 5.67 us -> 1.53 us
where the time goes in v9:
time: 99.9 us; the launch traced here: 99.7 us
  Pallas kernels  98.2 us (98%)
  local copies, waits for them, and re-layouts  1.53 us (2%)
    pallas_call x1, Pallas kernels, body(): pl.pallas_call(functools.partial(vcycle_kernel, n_parts, n_grp, reach, wi...  98.2 us

profile of v9, /device:TPU:32, one launch (start us, length us, event | category | flops | bytes accessed | tf_op | source)
XLA Modules:
  0.0 99.7 jit_solution(7402132796791964539)
XLA Ops:
  0.0 98.2 %shard_map.109 = f32[1,2,80,128]{3,2,1,0:T(8,128)} custom-call(f32[1,2,80,128]{3,2,1,0:T(8,128)} %rhs_hbm.1, f32[1,80,128]{2,1,0:T(8,128)} %absorption_hbm.1, f32[1,2,80,128]{3,2,1,0:T(8,128)} %vertical_hbm.1, f32[1,6,80,128]{3,2,1,0:T(8,128)} %horizontal_hbm.1, f32[1,80,128]{2,1,0:T(8,128)} %weights_hbm.1, s32[6,1,128]{2,1,0:T(1,128)} %bitcast.6, ...), custom_call_target="tpu_custom_call" | custom-call | tf_op jit(solution)/shard_map/pallas_call | solution.py:382
  98.2 1.5 %copy.13 = f32[1,2,80,128]{3,2,1,0:T(8,128)} copy(f32[1,2,80,128]{3,2,1,0:T(8,128)} %shard_map.109) | data formatting | bytes 163840

commit v10 on v9

--- a/solution.py
+++ b/solution.py
@@ -150,54 +150,58 @@
         hsum = hsum + jnp.abs(horizontal_v[0, n])
     diag_rows = diag_rows + hsum
     diag = jnp.where(live, to_cols(diag_rows), 1.0)
-    v0 = jnp.where(layer_lane == 0, 0.0, to_cols(vr0))
-    v1 = jnp.where(layer_lane == layers - 1, 0.0, to_cols(vr1))
-    h = [to_cols(horizontal_v[0, n]) for n in range(horizontal_v.shape[1])]
-    w = to_cols(weights_v[0])
+    inv_diag = 1.0 / diag
     rhs = jnp.concatenate([to_cols(rhs_v[0, t]) for t in range(tracers)], 1)
-
-    ext_rows = columns + halo
-    k_iota = lax.broadcasted_iota(jnp.int32, (ext_rows, columns), 0)
-    for n in range(n_nb):
-        chosen = jnp.transpose((k_iota == nb_v[n]).astype(F32)).astype(BF16)
-        rows = pl.ds(n * columns, columns)
-        mt_local[rows, :] = doubled(chosen[:, :columns])
-        mt_ghost[rows, :] = doubled(chosen[:, columns:])
     st_blocks = []
     for s in range(n_slots):
         block = (lax.broadcasted_iota(jnp.int32, (columns, width), 0) == si_v[0, s:s + 1, :]).astype(F32)
         st_blocks.append(jnp.transpose(block))
     st = doubled(jnp.concatenate(st_blocks, 0).astype(BF16))
-    at = (lax.broadcasted_iota(jnp.int32, (c1, columns), 0) == agg_v[...]).astype(F32)
-    a_full = jnp.transpose((lax.broadcasted_iota(jnp.int32, (LANES, columns), 0) == agg_v[...]).astype(F32))
-    a = doubled(a_full[:, :c1].astype(BF16))
-    coarse_rows = cext.shape[1]
-    n_crow = n_ch * c1
-    mct_blocks = []
-    for n in range(n_ch):
-        block = (lax.broadcasted_iota(jnp.int32, (coarse_rows, c1), 0) == cnb_v[n]).astype(F32)
-        mct_blocks.append(jnp.transpose(block))
-    mct = doubled(jnp.concatenate(mct_blocks, 0).astype(BF16))
-
-    widen = (
-        lax.broadcasted_iota(jnp.int32, (layers, LANES), 0) == lax.broadcasted_iota(jnp.int32, (layers, LANES), 1)
-    ).astype(F32)
-
-    def coarse_cols(slab):
-        return mm(slab, widen)
-
-    cvr0 = cvert_v[0, 0]
-    cvr1 = cvert_v[0, 1]
-    cdiag_rows = 0.5 + jnp.abs(cvr0) + jnp.abs(cvr1)
-    csum = jnp.abs(chor_v[0, 0])
-    for n in range(1, n_ch):
-        csum = csum + jnp.abs(chor_v[0, n])
-    cdiag = jnp.where(live, coarse_cols(cdiag_rows + csum), 1.0)
-    cv0 = jnp.where(layer_lane == 0, 0.0, coarse_cols(cvr0))
-    cv1 = jnp.where(layer_lane == layers - 1, 0.0, coarse_cols(cvr1))
-    ch = [coarse_cols(chor_v[0, n]) for n in range(n_ch)]
-    inv_diag = 1.0 / diag
-    inv_cdiag = 1.0 / cdiag
+    ctx = {}
+
+    def fine_setup():
+        ctx["v0"] = jnp.where(layer_lane == 0, 0.0, to_cols(vr0))
+        ctx["v1"] = jnp.where(layer_lane == layers - 1, 0.0, to_cols(vr1))
+        ctx["h"] = [to_cols(horizontal_v[0, n]) for n in range(horizontal_v.shape[1])]
+        k_iota = lax.broadcasted_iota(jnp.int32, (columns + halo, columns), 0)
+        for n in range(n_nb):
+            chosen = jnp.transpose((k_iota == nb_v[n]).astype(F32)).astype(BF16)
+            rows = pl.ds(n * columns, columns)
+            mt_local[rows, :] = doubled(chosen[:, :columns])
+            mt_ghost[rows, :] = doubled(chosen[:, columns:])
+
+    def coarse_setup():
+        ctx["w"] = to_cols(weights_v[0])
+        ctx["at"] = (lax.broadcasted_iota(jnp.int32, (c1, columns), 0) == agg_v[...]).astype(F32)
+        a_full = jnp.transpose((lax.broadcasted_iota(jnp.int32, (LANES, columns), 0) == agg_v[...]).astype(F32))
+        ctx["a"] = doubled(a_full[:, :c1].astype(BF16))
+        coarse_rows = cext.shape[1]
+        mct_blocks = []
+        for n in range(n_ch):
+            block = (lax.broadcasted_iota(jnp.int32, (coarse_rows, c1), 0) == cnb_v[n]).astype(F32)
+            mct_blocks.append(jnp.transpose(block))
+        ctx["mct"] = doubled(jnp.concatenate(mct_blocks, 0).astype(BF16))
+        widen = (
+            lax.broadcasted_iota(jnp.int32, (layers, LANES), 0) == lax.broadcasted_iota(jnp.int32, (layers, LANES), 1)
+        ).astype(F32)
+
+        def coarse_cols(slab):
+            return mm(slab, widen)
+
+        cvr0 = cvert_v[0, 0]
+        cvr1 = cvert_v[0, 1]
+        cdiag_rows = 0.5 + jnp.abs(cvr0) + jnp.abs(cvr1)
+        csum = jnp.abs(chor_v[0, 0])
+        for n in range(1, n_ch):
+            csum = csum + jnp.abs(chor_v[0, n])
+        cdiag = jnp.where(live, coarse_cols(cdiag_rows + csum), 1.0)
+        ctx["cdiag"] = cdiag
+        ctx["inv_cdiag"] = 1.0 / cdiag
+        ctx["cv0"] = jnp.where(layer_lane == 0, 0.0, coarse_cols(cvr0))
+        ctx["cv1"] = jnp.where(layer_lane == layers - 1, 0.0, coarse_cols(cvr1))
+        ctx["ch"] = [coarse_cols(chor_v[0, n]) for n in range(n_ch)]
+
+    setup_hooks = [fine_setup, coarse_setup]
 
     def halves(x):
         return [x[:, t * LANES:(t + 1) * LANES] for t in range(x.shape[1] // LANES)]
@@ -235,6 +239,9 @@
             @pl.when(valid(me + offsets[s]))
             def _():
                 fine_copy(slot, s).start()
+        if setup_hooks:
+            setup_hooks.pop(0)()
+        v0, v1, h = ctx["v0"], ctx["v1"], ctx["h"]
         local = select(mt_local[...], field)
         bases = []
         for t, part in enumerate(halves(field)):
@@ -274,6 +281,7 @@
         coarse_round[0] += 1
         finish_sends("coarse", coarse_copy)
         cext[slot, pl.ds(reach * c1, c1), :] = corr
+        cdiag, cv0, cv1, ch, mct = ctx["cdiag"], ctx["cv0"], ctx["cv1"], ctx["ch"], ctx["mct"]
         for k in by_distance:
             @pl.when(valid(me + offsets[k]))
             def _():
@@ -309,14 +317,14 @@
             step = OMEGA * (rhs - fine_apply(solution))
             solution = solution + per_half(step, inv_diag, lambda x, c: x * c)
         residual = rhs - fine_apply(solution)
-        weighted = per_half(residual, w, lambda x, c: x * c)
-        coarse_source = mm(at, weighted)
-        correction = per_half(OMEGA * coarse_source, inv_cdiag, lambda x, c: x * c)
+        weighted = per_half(residual, ctx["w"], lambda x, c: x * c)
+        coarse_source = mm(ctx["at"], weighted)
+        correction = per_half(OMEGA * coarse_source, ctx["inv_cdiag"], lambda x, c: x * c)
         for coarse_sweep_index in range(CSWEEPS - 1):
             step = OMEGA * (coarse_source - coarse_apply(correction))
-            correction = correction + per_half(step, inv_cdiag, lambda x, c: x * c)
-        lifted = select(a, correction)
-        solution = solution + per_half(lifted, w, lambda x, c: x * c)
+            correction = correction + per_half(step, ctx["inv_cdiag"], lambda x, c: x * c)
+        lifted = select(ctx["a"], correction)
+        solution = solution + per_half(lifted, ctx["w"], lambda x, c: x * c)
         for sweep_index in range(POST):
             step = OMEGA * (rhs - fine_apply(solution))
             solution = solution + per_half(step, inv_diag, lambda x, c: x * c)

time: 99.9 us -> 100 us (level)
  no operation moved by 1% of the time
where the time goes in v10:
time: 100 us; the launch traced here: 99.8 us
  Pallas kernels  98.3 us (98%)
  local copies, waits for them, and re-layouts  1.53 us (2%)
    pallas_call x1, Pallas kernels, body(): pl.pallas_call(functools.partial(vcycle_kernel, n_parts, n_grp, reach, wi...  98.3 us

profile of v10, /device:TPU:32, one launch (start us, length us, event | category | flops | bytes accessed | tf_op | source)
XLA Modules:
  0.0 99.8 jit_solution(17908676653440690168)
XLA Ops:
  0.0 98.3 %shard_map.109 = f32[1,2,80,128]{3,2,1,0:T(8,128)} custom-call(f32[1,2,80,128]{3,2,1,0:T(8,128)} %rhs_hbm.1, f32[1,80,128]{2,1,0:T(8,128)} %absorption_hbm.1, f32[1,2,80,128]{3,2,1,0:T(8,128)} %vertical_hbm.1, f32[1,6,80,128]{3,2,1,0:T(8,128)} %horizontal_hbm.1, f32[1,80,128]{2,1,0:T(8,128)} %weights_hbm.1, s32[6,1,128]{2,1,0:T(1,128)} %bitcast.6, ...), custom_call_target="tpu_custom_call" | custom-call | tf_op jit(solution)/shard_map/pallas_call | solution.py:390
  98.3 1.5 %copy.13 = f32[1,2,80,128]{3,2,1,0:T(8,128)} copy(f32[1,2,80,128]{3,2,1,0:T(8,128)} %shard_map.109) | data formatting | bytes 163840

commit v11 on v10

--- a/solution.py
+++ b/solution.py
@@ -62,7 +62,6 @@
     cnb_v,
     cvert_v,
     chor_v,
-    out_v,
     load_sem,
     mt_local,
     mt_ghost,
@@ -330,11 +329,12 @@
             solution = solution + per_half(step, inv_diag, lambda x, c: x * c)
     finish_sends("fine", fine_copy)
     finish_sends("coarse", coarse_copy)
-    for t, part in enumerate(halves(solution)):
-        out_v[0, t] = jnp.transpose(part)[:layers]
-    store = pltpu.make_async_copy(out_v, out_hbm, load_sem.at[len(loads)])
-    store.start()
-    store.wait()
+    out_hbm[...] = solution
+
+
+def unpack_kernel(layers, cols_ref, out_ref):
+    for t in range(out_ref.shape[1]):
+        out_ref[0, t] = jnp.transpose(cols_ref[:, t * LANES:(t + 1) * LANES])[:layers]
 
 
 def body(
@@ -375,8 +375,7 @@
     ext_rows = columns + n_slots * width
     coarse_rows = ext_rows
     scratch = [pltpu.VMEM(x.shape, x.dtype) for x in args] + [
-        pltpu.VMEM(right_side.shape, F32),
-        pltpu.SemaphoreType.DMA((len(args) + 1,)),
+        pltpu.SemaphoreType.DMA((len(args),)),
         pltpu.VMEM((neighbours.shape[1] * columns, 2 * columns), BF16),
         pltpu.VMEM((neighbours.shape[1] * columns, 2 * n_slots * width), BF16),
         pltpu.VMEM((2, n_slots * width, tracers * LANES), F32),
@@ -387,14 +386,20 @@
         pltpu.SemaphoreType.DMA((n_slots,)),
         pltpu.SemaphoreType.DMA((2, n_slots)),
     ]
-    return pl.pallas_call(
+    cols = pl.pallas_call(
         functools.partial(vcycle_kernel, n_parts, n_grp, reach, width),
-        out_shape=jax.ShapeDtypeStruct(right_side.shape, F32),
+        out_shape=jax.ShapeDtypeStruct((columns, tracers * LANES), F32),
         in_specs=[pl.BlockSpec(memory_space=pl.ANY)] * len(args),
-        out_specs=pl.BlockSpec(memory_space=pl.ANY),
+        out_specs=pl.BlockSpec(memory_space=pltpu.VMEM),
         scratch_shapes=scratch,
         compiler_params=pltpu.CompilerParams(collective_id=0, has_side_effects=True),
     )(*args)
+    return pl.pallas_call(
+        functools.partial(unpack_kernel, layers),
+        out_shape=jax.ShapeDtypeStruct(right_side.shape, F32),
+        in_specs=[pl.BlockSpec(memory_space=pltpu.VMEM)],
+        out_specs=pl.BlockSpec(memory_space=pltpu.VMEM),
+    )(cols)
 
 
 def solution(mesh):

time: 100 us -> 100 us (level)
  local copies, waits for them, and re-layouts: 1.53 us -> 0 us
  Pallas kernels: 98.3 us -> 99.8 us
    pallas_call x0 -> x1, Pallas kernels: none -> 1.63 us  [body(): pl.pallas_call(functools.partial(unpack_kernel, layers), out_shape=jax.Sh...]
    unnamed x1 -> x0, local copies, waits for them, and re-layouts: 1.53 us -> none
where the time goes in v11:
time: 100 us; the launch traced here: 99.8 us
  Pallas kernels  99.8 us (100%)
    pallas_call x1, Pallas kernels, body(): pl.pallas_call(functools.partial(vcycle_kernel, n_parts, n_grp, reach, wi...  98.2 us

profile of v11, /device:TPU:32, one launch (start us, length us, event | category | flops | bytes accessed | tf_op | source)
XLA Modules:
  0.0 99.8 jit_solution(17747023654818025701)
XLA Ops:
  0.0 98.2 %shard_map.109.cols_ref = f32[128,256]{1,0:T(8,128)} custom-call(f32[1,2,80,128]{3,2,1,0:T(8,128)} %rhs_hbm.1, f32[1,80,128]{2,1,0:T(8,128)} %absorption_hbm.1, f32[1,2,80,128]{3,2,1,0:T(8,128)} %vertical_hbm.1, f32[1,6,80,128]{3,2,1,0:T(8,128)} %horizontal_hbm.1, f32[1,80,128]{2,1,0:T(8,128)} %weights_hbm.1, s32[6,1,128]{2,1,0:T(1,128)} %bitcast.6, ...), custom_call_target="tpu_custom_call" | custom-call | tf_op jit(solution)/shard_map/pallas_call | solution.py:389
  98.2 1.6 %shard_map.110 = f32[1,2,80,128]{3,2,1,0:T(8,128)} custom-call(f32[128,256]{1,0:T(8,128)} %shard_map.109.cols_ref), custom_call_target="tpu_custom_call" | custom-call | tf_op jit(solution)/shard_map/pallas_call | solution.py:397

commit v12 on v10

--- a/solution.py
+++ b/solution.py
@@ -255,12 +255,14 @@
             @pl.when(valid(me - offsets[s]))
             def _():
                 fine_copy(slot, s).wait_recv()
-        gathered = select(mt_ghost[...], ghost[slot])
-        totals = []
-        for t, total in enumerate(bases):
-            for n in range(n_nb):
-                total = total + h[n] * gathered[n * columns:(n + 1) * columns, t * LANES:(t + 1) * LANES]
-            totals.append(total)
+        received = ghost[slot]
+        hi = received.astype(BF16)
+        stacked = jnp.concatenate([hi, (received - hi.astype(F32)).astype(BF16)], 0)
+        totals = list(bases)
+        for n in range(n_nb):
+            branch = jnp.dot(mt_ghost[pl.ds(n * columns, columns), :], stacked, preferred_element_type=F32)
+            for t in range(len(totals)):
+                totals[t] = totals[t] + h[n] * branch[:, t * LANES:(t + 1) * LANES]
         return jnp.concatenate(totals, 1)
 
     def coarse_copy(slot, k):

time: 100 us -> 100 us (level)
  no operation moved by 1% of the time
where the time goes in v12:
time: 100 us; the launch traced here: 99.8 us
  Pallas kernels  98.3 us (98%)
  local copies, waits for them, and re-layouts  1.53 us (2%)
    pallas_call x1, Pallas kernels, body(): pl.pallas_call(functools.partial(vcycle_kernel, n_parts, n_grp, reach, wi...  98.3 us

profile of v12, /device:TPU:32, one launch (start us, length us, event | category | flops | bytes accessed | tf_op | source)
XLA Modules:
  0.0 99.8 jit_solution(3892814766078068399)
XLA Ops:
  0.0 98.3 %shard_map.109 = f32[1,2,80,128]{3,2,1,0:T(8,128)} custom-call(f32[1,2,80,128]{3,2,1,0:T(8,128)} %rhs_hbm.1, f32[1,80,128]{2,1,0:T(8,128)} %absorption_hbm.1, f32[1,2,80,128]{3,2,1,0:T(8,128)} %vertical_hbm.1, f32[1,6,80,128]{3,2,1,0:T(8,128)} %horizontal_hbm.1, f32[1,80,128]{2,1,0:T(8,128)} %weights_hbm.1, s32[6,1,128]{2,1,0:T(1,128)} %bitcast.6, ...), custom_call_target="tpu_custom_call" | custom-call | tf_op jit(solution)/shard_map/pallas_call | solution.py:392
  98.3 1.5 %copy.13 = f32[1,2,80,128]{3,2,1,0:T(8,128)} copy(f32[1,2,80,128]{3,2,1,0:T(8,128)} %shard_map.109) | data formatting | bytes 163840

commit v13 on v10

--- a/solution.py
+++ b/solution.py
@@ -209,22 +209,21 @@
     def fine_copy(slot, s):
         rows = pl.ds(s * width, width)
         return pltpu.make_async_remote_copy(
-            src_ref=sendbuf.at[rows],
+            src_ref=sendbuf.at[slot, rows],
             dst_ref=ghost.at[slot, rows],
-            send_sem=send_sem.at[s],
+            send_sem=send_sem.at[slot, s],
             recv_sem=recv_sem.at[slot, s],
             device_id=device(me + offsets[s]),
             device_id_type=MESH,
         )
 
     fine_round = [0]
-    pending = {"fine": None, "coarse": None}
-
-    def finish_sends(kind, copy_of):
-        slot = pending[kind]
-        if slot is None:
+    pending = {("fine", 0): False, ("fine", 1): False, ("coarse", 0): False, ("coarse", 1): False}
+
+    def finish_sends(kind, copy_of, slot):
+        if not pending[(kind, slot)]:
             return
-        pending[kind] = None
+        pending[(kind, slot)] = False
         for s in range(n_slots):
             @pl.when(valid(me + offsets[s]))
             def _():
@@ -233,8 +232,8 @@
     def fine_apply(field):
         slot = fine_round[0] % 2
         fine_round[0] += 1
-        finish_sends("fine", fine_copy)
-        sendbuf[...] = select(st, field)
+        finish_sends("fine", fine_copy, slot)
+        sendbuf[slot] = select(st, field)
         for s in by_distance:
             @pl.when(valid(me + offsets[s]))
             def _():
@@ -250,7 +249,7 @@
             for n in range(n_nb):
                 total = total + h[n] * local[n * columns:(n + 1) * columns, t * LANES:(t + 1) * LANES]
             bases.append(total)
-        pending["fine"] = slot
+        pending[("fine", slot)] = True
         for s in range(n_slots):
             @pl.when(valid(me - offsets[s]))
             def _():
@@ -268,7 +267,7 @@
         return pltpu.make_async_remote_copy(
             src_ref=cext.at[slot, pl.ds(reach * c1, c1)],
             dst_ref=cext.at[slot, pl.ds((reach - d) * c1, c1)],
-            send_sem=csend_sem.at[k],
+            send_sem=csend_sem.at[slot, k],
             recv_sem=crecv_sem.at[slot, k],
             device_id=device(me + d),
             device_id_type=MESH,
@@ -279,7 +278,7 @@
     def coarse_apply(corr):
         slot = coarse_round[0] % 2
         coarse_round[0] += 1
-        finish_sends("coarse", coarse_copy)
+        finish_sends("coarse", coarse_copy, slot)
         cext[slot, pl.ds(reach * c1, c1), :] = corr
         cdiag, cv0, cv1, ch, mct = ctx["cdiag"], ctx["cv0"], ctx["cv1"], ctx["ch"], ctx["mct"]
         for k in by_distance:
@@ -290,7 +289,7 @@
         for part in halves(corr):
             lower, upper = shifted(part)
             bases.append(cdiag * part + cv0 * lower + cv1 * upper)
-        pending["coarse"] = slot
+        pending[("coarse", slot)] = True
         for k in range(n_slots):
             @pl.when(valid(me - offsets[k]))
             def _():
@@ -328,8 +327,9 @@
         for sweep_index in range(POST):
             step = OMEGA * (rhs - fine_apply(solution))
             solution = solution + per_half(step, inv_diag, lambda x, c: x * c)
-    finish_sends("fine", fine_copy)
-    finish_sends("coarse", coarse_copy)
+    for slot in range(2):
+        finish_sends("fine", fine_copy, slot)
+        finish_sends("coarse", coarse_copy, slot)
     for t, part in enumerate(halves(solution)):
         out_v[0, t] = jnp.transpose(part)[:layers]
     store = pltpu.make_async_copy(out_v, out_hbm, load_sem.at[len(loads)])
@@ -380,11 +380,11 @@
         pltpu.VMEM((neighbours.shape[1] * columns, 2 * columns), BF16),
         pltpu.VMEM((neighbours.shape[1] * columns, 2 * n_slots * width), BF16),
         pltpu.VMEM((2, n_slots * width, tracers * LANES), F32),
-        pltpu.VMEM((n_slots * width, tracers * LANES), F32),
+        pltpu.VMEM((2, n_slots * width, tracers * LANES), F32),
         pltpu.VMEM((2, coarse_rows, tracers * LANES), F32),
-        pltpu.SemaphoreType.DMA((n_slots,)),
         pltpu.SemaphoreType.DMA((2, n_slots)),
-        pltpu.SemaphoreType.DMA((n_slots,)),
+        pltpu.SemaphoreType.DMA((2, n_slots)),
+        pltpu.SemaphoreType.DMA((2, n_slots)),
         pltpu.SemaphoreType.DMA((2, n_slots)),
     ]
     return pl.pallas_call(

time: 100 us -> 100 us (level)
  no operation moved by 1% of the time
where the time goes in v13:
time: 100 us; the launch traced here: 99.9 us
  Pallas kernels  98.4 us (98%)
  local copies, waits for them, and re-layouts  1.53 us (2%)
    pallas_call x1, Pallas kernels, body(): pl.pallas_call(functools.partial(vcycle_kernel, n_parts, n_grp, reach, wi...  98.4 us

profile of v13, /device:TPU:32, one launch (start us, length us, event | category | flops | bytes accessed | tf_op | source)
XLA Modules:
  0.0 99.9 jit_solution(10601802412160998547)
XLA Ops:
  0.0 98.4 %shard_map.109 = f32[1,2,80,128]{3,2,1,0:T(8,128)} custom-call(f32[1,2,80,128]{3,2,1,0:T(8,128)} %rhs_hbm.1, f32[1,80,128]{2,1,0:T(8,128)} %absorption_hbm.1, f32[1,2,80,128]{3,2,1,0:T(8,128)} %vertical_hbm.1, f32[1,6,80,128]{3,2,1,0:T(8,128)} %horizontal_hbm.1, f32[1,80,128]{2,1,0:T(8,128)} %weights_hbm.1, s32[6,1,128]{2,1,0:T(1,128)} %bitcast.6, ...), custom_call_target="tpu_custom_call" | custom-call | tf_op jit(solution)/shard_map/pallas_call | solution.py:390
  98.4 1.5 %copy.13 = f32[1,2,80,128]{3,2,1,0:T(8,128)} copy(f32[1,2,80,128]{3,2,1,0:T(8,128)} %shard_map.109) | data formatting | bytes 163840

commit v14 on v10

--- a/solution.py
+++ b/solution.py
@@ -234,11 +234,16 @@
         slot = fine_round[0] % 2
         fine_round[0] += 1
         finish_sends("fine", fine_copy)
-        sendbuf[...] = select(st, field)
-        for s in by_distance:
-            @pl.when(valid(me + offsets[s]))
-            def _():
-                fine_copy(slot, s).start()
+        hi = field.astype(BF16)
+        stacked = jnp.concatenate([hi, (field - hi.astype(F32)).astype(BF16)], 0)
+        for group in (by_distance[:2], by_distance[2:]):
+            for s in group:
+                rows = pl.ds(s * width, width)
+                sendbuf[rows, :] = jnp.dot(st[s * width:(s + 1) * width], stacked, preferred_element_type=F32)
+            for s in group:
+                @pl.when(valid(me + offsets[s]))
+                def _():
+                    fine_copy(slot, s).start()
         if setup_hooks:
             setup_hooks.pop(0)()
         v0, v1, h = ctx["v0"], ctx["v1"], ctx["h"]

time: 100 us -> 99.6 us (level)
  no operation moved by 1% of the time
where the time goes in v14:
time: 99.6 us; the launch traced here: 99.5 us
  Pallas kernels  97.9 us (98%)
  local copies, waits for them, and re-layouts  1.53 us (2%)
    pallas_call x1, Pallas kernels, body(): pl.pallas_call(functools.partial(vcycle_kernel, n_parts, n_grp, reach, wi...  97.9 us

profile of v14, /device:TPU:32, one launch (start us, length us, event | category | flops | bytes accessed | tf_op | source)
XLA Modules:
  0.0 99.5 jit_solution(4908699177205879664)
XLA Ops:
  0.0 97.9 %shard_map.109 = f32[1,2,80,128]{3,2,1,0:T(8,128)} custom-call(f32[1,2,80,128]{3,2,1,0:T(8,128)} %rhs_hbm.1, f32[1,80,128]{2,1,0:T(8,128)} %absorption_hbm.1, f32[1,2,80,128]{3,2,1,0:T(8,128)} %vertical_hbm.1, f32[1,6,80,128]{3,2,1,0:T(8,128)} %horizontal_hbm.1, f32[1,80,128]{2,1,0:T(8,128)} %weights_hbm.1, s32[6,1,128]{2,1,0:T(1,128)} %bitcast.6, ...), custom_call_target="tpu_custom_call" | custom-call | tf_op jit(solution)/shard_map/pallas_call | solution.py:395
  97.9 1.5 %copy.13 = f32[1,2,80,128]{3,2,1,0:T(8,128)} copy(f32[1,2,80,128]{3,2,1,0:T(8,128)} %shard_map.109) | data formatting | bytes 163840

commit v15 on v14

--- a/solution.py
+++ b/solution.py
@@ -231,15 +231,18 @@
                 copy_of(slot, s).wait_send()
 
     def fine_apply(field):
+        first = fine_round[0] == 0
         slot = fine_round[0] % 2
         fine_round[0] += 1
         finish_sends("fine", fine_copy)
         hi = field.astype(BF16)
         stacked = jnp.concatenate([hi, (field - hi.astype(F32)).astype(BF16)], 0)
-        for group in (by_distance[:2], by_distance[2:]):
+        for group in (by_distance,) if first else (by_distance[:2], by_distance[2:]):
             for s in group:
                 rows = pl.ds(s * width, width)
                 sendbuf[rows, :] = jnp.dot(st[s * width:(s + 1) * width], stacked, preferred_element_type=F32)
+            if first:
+                pl.semaphore_wait(barrier, peers)
             for s in group:
                 @pl.when(valid(me + offsets[s]))
                 def _():
@@ -309,7 +312,6 @@
         return jnp.concatenate(totals, 1)
 
     peers = sum(valid(me + d).astype(jnp.int32) for d in offsets)
-    pl.semaphore_wait(barrier, peers)
 
     def per_half(x, coeff, op):
         return jnp.concatenate([op(part, coeff) for part in halves(x)], 1)

time: 99.6 us -> 99.5 us (level)
  no operation moved by 1% of the time
where the time goes in v15:
time: 99.5 us; the launch traced here: 99.3 us
  Pallas kernels  97.8 us (98%)
  local copies, waits for them, and re-layouts  1.53 us (2%)
    pallas_call x1, Pallas kernels, body(): pl.pallas_call(functools.partial(vcycle_kernel, n_parts, n_grp, reach, wi...  97.8 us

profile of v15, /device:TPU:32, one launch (start us, length us, event | category | flops | bytes accessed | tf_op | source)
XLA Modules:
  0.0 99.3 jit_solution(14880813320218199587)
XLA Ops:
  0.0 97.8 %shard_map.109 = f32[1,2,80,128]{3,2,1,0:T(8,128)} custom-call(f32[1,2,80,128]{3,2,1,0:T(8,128)} %rhs_hbm.1, f32[1,80,128]{2,1,0:T(8,128)} %absorption_hbm.1, f32[1,2,80,128]{3,2,1,0:T(8,128)} %vertical_hbm.1, f32[1,6,80,128]{3,2,1,0:T(8,128)} %horizontal_hbm.1, f32[1,80,128]{2,1,0:T(8,128)} %weights_hbm.1, s32[6,1,128]{2,1,0:T(1,128)} %bitcast.6, ...), custom_call_target="tpu_custom_call" | custom-call | tf_op jit(solution)/shard_map/pallas_call | solution.py:397
  97.8 1.5 %copy.13 = f32[1,2,80,128]{3,2,1,0:T(8,128)} copy(f32[1,2,80,128]{3,2,1,0:T(8,128)} %shard_map.109) | data formatting | bytes 163840

commit v16 on v15

--- a/solution.py
+++ b/solution.py
@@ -250,7 +250,7 @@
         if setup_hooks:
             setup_hooks.pop(0)()
         v0, v1, h = ctx["v0"], ctx["v1"], ctx["h"]
-        local = select(mt_local[...], field)
+        local = jnp.dot(mt_local[...], stacked, preferred_element_type=F32)
         bases = []
         for t, part in enumerate(halves(field)):
             lower, upper = shifted(part)

time: 99.5 us -> 99.5 us (level)
  no operation moved by 1% of the time
where the time goes in v16:
time: 99.5 us; the launch traced here: 99.3 us
  Pallas kernels  97.8 us (98%)
  local copies, waits for them, and re-layouts  1.53 us (2%)
    pallas_call x1, Pallas kernels, body(): pl.pallas_call(functools.partial(vcycle_kernel, n_parts, n_grp, reach, wi...  97.8 us

profile of v16, /device:TPU:32, one launch (start us, length us, event | category | flops | bytes accessed | tf_op | source)
XLA Modules:
  0.0 99.3 jit_solution(14880813320218199587)
XLA Ops:
  0.0 97.8 %shard_map.109 = f32[1,2,80,128]{3,2,1,0:T(8,128)} custom-call(f32[1,2,80,128]{3,2,1,0:T(8,128)} %rhs_hbm.1, f32[1,80,128]{2,1,0:T(8,128)} %absorption_hbm.1, f32[1,2,80,128]{3,2,1,0:T(8,128)} %vertical_hbm.1, f32[1,6,80,128]{3,2,1,0:T(8,128)} %horizontal_hbm.1, f32[1,80,128]{2,1,0:T(8,128)} %weights_hbm.1, s32[6,1,128]{2,1,0:T(1,128)} %bitcast.6, ...), custom_call_target="tpu_custom_call" | custom-call | tf_op jit(solution)/shard_map/pallas_call | solution.py:397
  97.8 1.5 %copy.13 = f32[1,2,80,128]{3,2,1,0:T(8,128)} copy(f32[1,2,80,128]{3,2,1,0:T(8,128)} %shard_map.109) | data formatting | bytes 163840
